TPU v7x, 512 devices: a whole 4x8x8 slice. The times are simulated.
512 devices in a mesh: seq: 8 (over z_hi, core), head: 16 (over z_lo, y), dp: 4 (over x).
Axes of the slice: x: 4, y: 8, z: 8 (z_hi: 4, z_lo: 2; z = z_hi * 2 + z_lo), core: 2. Of those that a mesh axis runs over, the one named last changes fastest.
Arguments:
- tokens: bfloat16 [4, 1024, 4096], P('dp', 'seq', 'head'), may hold values from -6 to 6
- w_qkv: bfloat16 [4096, 3, 2048], P(('seq', 'dp'), None, 'head'), may hold values from -0.09375 to 0.09375
- w_lr: bfloat16 [4096, 16], P(None, 'head'), may hold values from -0.1875 to 0.1875
- w_out: bfloat16 [4096, 2048], P(('seq', 'dp'), 'head'), may hold values from -0.125 to 0.125
- w1_init: float32 [16, 128, 512], P('head'), may hold values from -0.5 to 0.5
- w2_init: float32 [16, 512, 128], P('head'), may hold values from -0.25 to 0.25
- d_out: bfloat16 [4, 1024, 4096], P('dp', 'seq', 'head'), may hold values from -6 to 6
Outputs:
- out: bfloat16 [4, 1024, 4096], P('dp', 'seq', 'head')
- d_tokens: bfloat16 [4, 1024, 4096], P('dp', 'seq', 'head')
- d_w1_init: float32 [16, 128, 512], P('head', None, ('seq', 'dp'))
- d_w2_init: float32 [16, 512, 128], P('head', ('seq', 'dp'))
All inputs are finite; a program needn't handle non-finite values.
Results may differ from a plain program's by a relative error of at most 0.018.
Values may be sent and summed in bfloat16 or wider, within the bound.
A program may use at most 64 MiB of HBM per device.

v0:
```python
import math

import jax
import jax.numpy as jnp
from jax import lax
from jax.sharding import PartitionSpec as P

MB = 64


EPSILON = 1e-06
BASE_RATE = 0.1
GELU_SCALE = 0.7978845608028654
GELU_CUBIC = 0.044715
CONTRACT_LAST = (((1,), (1,)), ((), ()))
CONTRACT_FIRST = (((0,), (0,)), ((), ()))


def joined_along(parts, dim):
    parts = jnp.moveaxis(parts, 0, dim)
    lengths = parts.shape
    return parts.reshape(*lengths[:dim], lengths[dim] * lengths[dim + 1], *lengths[dim + 2 :])


def from_everyone(array, axis):
    copies = jnp.broadcast_to(array, (lax.axis_size(axis), *array.shape))
    return lax.all_to_all(copies, axis, split_axis=0, concat_axis=0, tiled=True)


def gather_directly(array, axis, dim):
    return joined_along(from_everyone(array, axis), dim)


def in_one_piece(arrays, axis, dim, along):
    widths = [math.prod(a.shape[along:]) for a in arrays]
    both = jnp.concatenate(
        [a.reshape(*a.shape[:along], w) for a, w in zip(arrays, widths)], axis=along
    )
    out = lax.all_gather(both, axis, axis=dim, tiled=True)
    parts = jnp.split(out, [sum(widths[:k]) for k in range(1, len(widths))], axis=along)
    return tuple((b.reshape(*out.shape[:along], *a.shape[along:]) for a, b in zip(arrays, parts)))


def in_blocks(array, dim, peers):
    before, after = (array.shape[:dim], array.shape[dim + 1 :])
    return jnp.moveaxis(array.reshape(*before, peers, -1, *after), dim, 0)


def summed_on_arrival(array, axis, dim):
    peers = lax.axis_size(axis)
    parts = lax.all_to_all(in_blocks(array, dim, peers), axis, 0, 0, tiled=True)
    return jnp.sum(parts.astype(jnp.float32), axis=0)


def shifted(array, axis, by):
    peers = lax.axis_size(axis)
    pairs = [(i, i + by) for i in range(peers) if 0 <= i + by < peers]
    return lax.ppermute(array, axis, pairs)


def side_by_side(arrays, axis, dim, along):
    widths = [a.shape[along] for a in arrays]
    both = jnp.concatenate(arrays, axis=along)
    out = lax.psum_scatter(both, axis, scatter_dimension=dim, tiled=True)
    return tuple(jnp.split(out, [sum(widths[:k]) for k in range(1, len(widths))], axis=along))


def gelu_value(inputs):
    bend = jnp.tanh(GELU_SCALE * (inputs + GELU_CUBIC * inputs * inputs * inputs))
    return 0.5 * inputs * (1.0 + bend)


def gelu_slope(inputs):
    bend = jnp.tanh(GELU_SCALE * (inputs + GELU_CUBIC * inputs * inputs * inputs))
    return 0.5 * (1.0 + bend) + 0.5 * inputs * (1.0 - bend * bend) * GELU_SCALE * (
        1.0 + 3.0 * GELU_CUBIC * inputs * inputs
    )


def float_dot(left, right):
    return jnp.dot(left, right)


def float_dims(left, right, dims):
    return lax.dot_general(left, right, dims)


def norm_rows(inputs):
    centred = inputs - jnp.mean(inputs, axis=-1, keepdims=True)
    inv_scale = lax.rsqrt(jnp.mean(centred * centred, axis=-1, keepdims=True) + EPSILON)
    return (centred * inv_scale, inv_scale)


def local_grads(w_first, w_second, key_rows, value_rows):
    pre_first = float_dot(key_rows, w_first)
    hidden = gelu_value(pre_first)
    normed, inv_scale = norm_rows(float_dot(hidden, w_second))
    residual = normed - (value_rows - key_rows)
    grad_second = inv_scale * (
        residual
        - jnp.mean(residual, axis=-1, keepdims=True)
        - normed * jnp.mean(residual * normed, axis=-1, keepdims=True)
    )
    grad_first = float_dims(grad_second, w_second, CONTRACT_LAST) * gelu_slope(pre_first)
    return (hidden, grad_first, grad_second)


def inner_update(w_first, w_second, key_rows, hidden, grad_first, grad_second, rates):
    new_first = w_first - float_dims(key_rows, grad_first * rates[:, None], CONTRACT_FIRST)
    new_second = w_second - float_dims(hidden, grad_second * rates[:, None], CONTRACT_FIRST)
    return (new_first, new_second)


def inner_block(state_carry, block_rows):
    w_first, w_second = state_carry
    queries, key_rows, value_rows, rate_logit = block_rows
    rates = BASE_RATE * jax.nn.sigmoid(rate_logit) / key_rows.shape[1]
    hidden, grad_first, grad_second = local_grads(w_first, w_second, key_rows, value_rows)
    size_block = key_rows.shape[0]
    positions = lax.broadcasted_iota(jnp.int32, (size_block, size_block), 0)
    sources = lax.broadcasted_iota(jnp.int32, (size_block, size_block), 1)
    causal = jnp.where(sources <= positions, rates[None, :], jnp.float32(0.0))
    mix_first = float_dims(queries, key_rows, CONTRACT_LAST) * causal
    pre_query = float_dot(queries, w_first) - float_dot(mix_first, grad_first)
    hidden_query = gelu_value(pre_query)
    mix_second = float_dims(hidden_query, hidden, CONTRACT_LAST) * causal
    normed, unused = norm_rows(
        float_dot(hidden_query, w_second) - float_dot(mix_second, grad_second)
    )
    new_state = inner_update(w_first, w_second, key_rows, hidden, grad_first, grad_second, rates)
    return (new_state, queries + normed)


def inner_state(state_carry, block_rows):
    w_first, w_second = state_carry
    key_rows, value_rows, rate_logit = block_rows
    rates = BASE_RATE * jax.nn.sigmoid(rate_logit) / key_rows.shape[1]
    hidden, grad_first, grad_second = local_grads(w_first, w_second, key_rows, value_rows)
    return (inner_update(w_first, w_second, key_rows, hidden, grad_first, grad_second, rates), None)


def inner_run(w_first, w_second, queries, key_rows, value_rows, rate_logit):
    row_count = queries.shape[0]
    blocks = row_count // MB
    shaped = (
        queries.reshape(blocks, MB, -1),
        key_rows.reshape(blocks, MB, -1),
        value_rows.reshape(blocks, MB, -1),
        rate_logit.reshape(blocks, MB),
    )
    final_state, outputs = lax.scan(inner_block, (w_first, w_second), shaped)
    return (final_state[0], final_state[1], outputs.reshape(row_count, -1))


def inner_replay(w_first, w_second, key_rows, value_rows, rate_logit):
    row_count = key_rows.shape[0]
    blocks = row_count // MB
    shaped = (
        key_rows.reshape(blocks, MB, -1),
        value_rows.reshape(blocks, MB, -1),
        rate_logit.reshape(blocks, MB),
    )
    final_state, unused = lax.scan(inner_state, (w_first, w_second), shaped)
    return final_state


def body(tokens, w_qkv, w_lr, w_out, w1_init, w2_init, d_out):
    head_width = w_qkv.shape[2]
    features = gather_directly(tokens[0], "head", 1)
    part_qkv, part_out = in_one_piece((w_qkv, w_out), "dp", 0, 1)
    wide_qkv, wide_out = in_one_piece((part_qkv, part_out), "seq", 0, 1)
    full_depth = wide_qkv.shape[0]
    qkv_matrix = wide_qkv.reshape(full_depth, 3 * head_width)
    projected = jnp.dot(features, qkv_matrix, preferred_element_type=jnp.float32)
    rate_logit = jnp.dot(features, w_lr, preferred_element_type=jnp.float32)[:, 0]
    queries = projected[:, :head_width]
    key_rows = projected[:, head_width : 2 * head_width]
    value_rows = projected[:, 2 * head_width :]
    seq_place = lax.axis_index("seq")
    seq_count = lax.axis_size("seq")
    start_first = w1_init[0]
    start_second = w2_init[0]
    gathered = in_one_piece((key_rows, value_rows, rate_logit), "seq", 0, 1)
    row_count = queries.shape[0]

    def replay_turn(turn_index, state_carry):
        offset = turn_index * row_count
        key_part = lax.dynamic_slice_in_dim(gathered[0], offset, row_count, 0)
        value_part = lax.dynamic_slice_in_dim(gathered[1], offset, row_count, 0)
        logit_part = lax.dynamic_slice_in_dim(gathered[2], offset, row_count, 0)
        return inner_replay(state_carry[0], state_carry[1], key_part, value_part, logit_part)

    in_first, in_second = lax.fori_loop(0, seq_place, replay_turn, (start_first, start_second))
    results, pull = jax.vjp(
        inner_run, in_first, in_second, queries, key_rows, value_rows, rate_logit
    )
    own_out = results[2]
    ttt_out = own_out.astype(jnp.bfloat16)
    out_term = lax.dot_general(ttt_out, wide_out, CONTRACT_LAST, preferred_element_type=jnp.float32)
    out_sum = summed_on_arrival(out_term.astype(jnp.bfloat16), "head", 1)
    out = out_sum.astype(jnp.bfloat16)[None]
    d_full = gather_directly(d_out[0], "head", 1)
    d_ttt = jnp.dot(d_full, wide_out, preferred_element_type=jnp.float32)

    def pull_piece(state_carry):
        return pull((state_carry[0], state_carry[1], d_ttt))

    def keep_grads(state_carry):
        return state_carry

    zero_grads = (
        jnp.zeros_like(start_first),
        jnp.zeros_like(start_second),
        jnp.zeros_like(queries),
        jnp.zeros_like(key_rows),
        jnp.zeros_like(value_rows),
        jnp.zeros_like(rate_logit),
    )

    def backward_turn(step_index, state_carry):
        active = seq_place == seq_count - 1 - step_index
        result = lax.cond(active, pull_piece, keep_grads, state_carry)
        back_first, back_second = shifted((result[0], result[1]), "seq", -1)
        return (back_first, back_second, result[2], result[3], result[4], result[5])

    carried = lax.fori_loop(0, seq_count - 1, backward_turn, zero_grads)
    is_first = seq_place == 0
    result = lax.cond(is_first, pull_piece, keep_grads, carried)
    masked_first = jnp.where(is_first, result[0], jnp.float32(0.0)).transpose(1, 0)
    masked_second = jnp.where(is_first, result[1], jnp.float32(0.0))
    share_first, share_second = side_by_side((masked_first, masked_second), ("seq", "dp"), 0, 1)
    d_proj = jnp.concatenate([result[2], result[3], result[4]], axis=1).astype(jnp.bfloat16)
    grad_term = lax.dot_general(
        d_proj, qkv_matrix, CONTRACT_LAST, preferred_element_type=jnp.float32
    )
    grad_term = grad_term + result[5][:, None] * w_lr[:, 0].astype(jnp.float32)[None, :]
    grad_sum = summed_on_arrival(grad_term.astype(jnp.bfloat16), "head", 1)
    d_tokens = grad_sum.astype(jnp.bfloat16)[None]
    return (out, d_tokens, share_first.transpose(1, 0)[None], share_second[None])


def solution(mesh):
    placed = (
        P("dp", "seq", "head"),
        P(("seq", "dp"), None, "head"),
        P(None, "head"),
        P(("seq", "dp"), "head"),
        P("head", None, None),
        P("head", None, None),
        P("dp", "seq", "head"),
    )
    return jax.shard_map(
        body,
        mesh=mesh,
        in_specs=placed,
        out_specs=(
            P("dp", "seq", "head"),
            P("dp", "seq", "head"),
            P("head", None, ("seq", "dp")),
            P("head", ("seq", "dp"), None),
        ),
        check_vma=False,
    )
```

profile of v0, /device:TPU:1, one launch (start us, length us, event | category | flops | bytes accessed | tf_op | source)
XLA Modules:
  0.0 675.1 jit_solution(17109548624758123038)
XLA Ops:
  9.1 13.7 %all_gather.9 = bf16[512,512]{0,1:T(8,128)(2,1)} all-gather(bf16[128,512]{0,1:T(8,128)(2,1)S(1)} %pad_maximum_fusion.2), channel_id=1, replica_groups=mesh['seq'=8,'head'=16,'dp'=4] {'dp'}, dimensions={0}, use_global_device_ids=true | all-gather | bytes 655360 | tf_op jit(solution)/shard_map/all_gather | solution.py:39
  25.0 8.2 %all-to-all-start = ((bf16[16,128,256]{1,2,0:T(8,128)(2,1)}), bf16[16,128,256]{1,2,0:T(8,128)(2,1)S(1)}, u32[]{:S(2)}, u32[]{:S(2)}) async-start(bf16[16,128,256]{1,2,0:T(8,128)(2,1)} %broadcast_in_dim.637), calls=%async_computation | async-start | bytes 2097152 | tf_op jit(solution)/shard_map/all_to_all | solution.py:27
  33.4 23.5 %all-to-all-done = bf16[16,128,256]{1,2,0:T(8,128)(2,1)S(1)} async-done(((bf16[16,128,256]{1,2,0:T(8,128)(2,1)}), bf16[16,128,256]{1,2,0:T(8,128)(2,1)S(1)}, u32[]{:S(2)}, u32[]{:S(2)}) %all-to-all-start) | async-done | bytes 1048608 | tf_op jit(solution)/shard_map/all_to_all | solution.py:27
  58.1 6.6 all-to-all-start.2
  65.1 38.7 %all-gather.3.cloned.1.call-done = bf16[4096,512]{0,1:T(8,128)(2,1)} async-done(((bf16[512,512]{0,1:T(8,128)(2,1)}), bf16[4096,512]{0,1:T(8,128)(2,1)}) %all-gather.3.cloned.1.call-update) | async-done | bytes 4194320 | tf_op jit(solution)/shard_map/all_gather | solution.py:39
  103.8 2.9 fusion.427
  114.7 26.4 %all-gather.5.cloned.1.call-done = f32[1024,257]{1,0:T(8,128)} async-done(((f32[128,257]{1,0:T(8,128)}), f32[1024,257]{1,0:T(8,128)}) %all-gather.5.cloned.1.call-update) | async-done | bytes 1052688 | tf_op jit(solution)/shard_map/all_gather | solution.py:39
  145.3 11.3 %while.221 = (s32[]{:T(128)}, f32[128,512]{1,0:T(8,128)S(1)}, f32[512,128]{1,0:T(8,128)S(1)}, s32[]{:T(128)}, f32[1024,128]{1,0:T(8,128)}, /*index=5*/f32[1024,1...) while((s32[]{:T(128)}, f32[128,512]{1,0:T(8,128)S(1)}, ...), condition=%wide.region_7.8_spmd, body=%wide.region_0.7_spmd.sunk | while | flops 43450692 | bytes 3517540 | solution.py:193
  148.2 8.4 %while.224 = (s32[]{:T(128)}, f32[128,512]{1,0:T(8,128)S(1)}, f32[512,128]{1,0:T(8,128)S(1)}, f32[2,64,128]{2,1,0:T(8,128)S(1)}, f32[2,64,128]{2,1,0:T(8,128)}, /*index=5*/f32[2,64]{1,0:T(2,128)}, s32[]{:T(128)}) while((s32[]{:T(128)}, f32[128,512]{1,0:T(8,128)S(1)}, f32[512,128]{1,0:T(8,128)S(1)}, f32[2,64,128]{2,1,0:T(8,128)S(1)}, ...), condition=%wide.region_6.6_spmd, body=%wide.region_1.5_spmd.sunk | while | flops 43450688 | bytes 3253113 | solution.py:163
  156.6 21.9 %while.223 = (s32[]{:T(128)}, f32[128,512]{1,0:T(8,128)S(1)}, f32[512,128]{1,0:T(8,128)S(1)}, bf16[2,64,128]{2,1,0:T(8,128)(2,1)}, f32[2,64]{1,0:T(2,128)}, /*in...) while((s32[]{:T(128)}, f32[128,512]{1,0:T(8,128)S(1)}, ...), condition=%wide.region_15.16_spmd.clone.clone, body=%wide.region_8.15_spmd.clone.clone.sunk | while | flops 72078464 | bytes 24311264 | solution.py:151
  181.0 321.6 %while.222 = (s32[]{:T(128)}, f32[128,512]{1,0:T(8,128)S(1)}, f32[512,128]{1,0:T(8,128)S(1)}, bf16[128,128]{1,0:T(8,128)(2,1)}, bf16[128,128]{1,0:T(8,128)(2,1)}...) while((s32[]{:T(128)}, f32[128,512]{1,0:T(8,128)S(1)}, ...), condition=%wide.region_32.33_spmd.clone, body=%wide.region_17.32_spmd.clone.sunk | while | flops 141779328 | bytes 26241492 | solution.py:226
  184.9 20.5 %collective-permute-done = f32[128,512]{1,0:T(8,128)} collective-permute-done((f32[128,512]{1,0:T(8,128)S(1)}, f32[128,512]{1,0:T(8,128)}, u32[]{:S(2)}, u32[]{:S(2)}) %collective-permute-start) | collective-permute-done | bytes 262176 | tf_op jit(solution)/shard_map/while/body/eval_jaxpr/ppermute | solution.py:58
  212.1 9.9 %collective-permute-done = f32[128,512]{1,0:T(8,128)} collective-permute-done((f32[128,512]{1,0:T(8,128)S(1)}, f32[128,512]{1,0:T(8,128)}, u32[]{:S(2)}, u32[]{:S(2)}) %collective-permute-start) | collective-permute-done | bytes 262176 | tf_op jit(solution)/shard_map/while/body/eval_jaxpr/ppermute | solution.py:58
  228.6 15.2 %collective-permute-done = f32[128,512]{1,0:T(8,128)} collective-permute-done((f32[128,512]{1,0:T(8,128)S(1)}, f32[128,512]{1,0:T(8,128)}, u32[]{:S(2)}, u32[]{:S(2)}) %collective-permute-start) | collective-permute-done | bytes 262176 | tf_op jit(solution)/shard_map/while/body/eval_jaxpr/ppermute | solution.py:58
  250.5 9.8 %collective-permute-done = f32[128,512]{1,0:T(8,128)} collective-permute-done((f32[128,512]{1,0:T(8,128)S(1)}, f32[128,512]{1,0:T(8,128)}, u32[]{:S(2)}, u32[]{:S(2)}) %collective-permute-start) | collective-permute-done | bytes 262176 | tf_op jit(solution)/shard_map/while/body/eval_jaxpr/ppermute | solution.py:58
  266.9 15.0 %collective-permute-done = f32[128,512]{1,0:T(8,128)} collective-permute-done((f32[128,512]{1,0:T(8,128)S(1)}, f32[128,512]{1,0:T(8,128)}, u32[]{:S(2)}, u32[]{:S(2)}) %collective-permute-start) | collective-permute-done | bytes 262176 | tf_op jit(solution)/shard_map/while/body/eval_jaxpr/ppermute | solution.py:58
  288.6 172.6 %collective-permute-done = f32[128,512]{1,0:T(8,128)} collective-permute-done((f32[128,512]{1,0:T(8,128)S(1)}, f32[128,512]{1,0:T(8,128)}, u32[]{:S(2)}, u32[]{:S(2)}) %collective-permute-start) | collective-permute-done | bytes 262176 | tf_op jit(solution)/shard_map/while/body/eval_jaxpr/ppermute | solution.py:58
  463.9 27.3 %conditional.5 = ((f32[128,512]{1,0:T(8,128)S(1)}, f32[512,128]{1,0:T(8,128)S(1)}, bf16[128,128]{1,0:T(8,128)(2,1)}, bf16[128,128]{1,0:T(8,128)(2,1)}, bf16[128,128]{1,0:T(8,128)(2,1)}, /*index=5*/f32[128]{0:T(128)})) conditional(s32[]{:T(128)} %convert_element_type.45, (f32[128,512]{1,0:T(8,128)S(1)}, f32[512,128]{1,0:T(8,128)S(1)}, ...), branch_computations={%region_18.18_spmd, %region_19.31_spmd} | conditional | flops 141779328 | bytes 23061956 | solution.py:222
  466.4 23.5 %while.218 = (s32[]{:T(128)}, f32[128,512]{1,0:T(8,128)S(1)}, f32[512,128]{1,0:T(8,128)S(1)}, bf16[2,64,128]{2,1,0:T(8,128)(2,1)}, bf16[2,64,128]{2,1,0:T(8,128)...) while((s32[]{:T(128)}, f32[128,512]{1,0:T(8,128)S(1)}, ...), condition=%wide.region_31.30_spmd, body=%wide.region_20.29_spmd.sunk | while | flops 141775232 | bytes 22924716 | solution.py:151
  495.0 4.8 collective-permute-done
  506.4 7.1 %all-to-all-start.3 = ((bf16[16,128,256]{2,1,0:T(8,128)(2,1)}), bf16[16,128,256]{2,1,0:T(8,128)(2,1)S(1)}, u32[]{:S(2)}, u32[]{:S(2)}) async-start(bf16[16,128,256]{2,1,0:T(8,128)(2,1)} %bitcast.946), calls=%async_computation.3 | async-start | bytes 2097152 | tf_op jit(solution)/shard_map/all_to_all | solution.py:51
  516.3 13.0 %all-to-all-done.3 = bf16[16,128,256]{2,1,0:T(8,128)(2,1)S(1)} async-done(((bf16[16,128,256]{2,1,0:T(8,128)(2,1)}), bf16[16,128,256]{2,1,0:T(8,128)(2,1)S(1)}, u32[]{:S(2)}, u32[]{:S(2)}) %all-to-all-start.3) | async-done | bytes 1048608 | tf_op jit(solution)/shard_map/all_to_all | solution.py:51
  529.2 4.5 all-to-all-start.1
  534.8 130.9 %reduce-scatter.2.cloned.1.call-done = f32[16,256]{1,0:T(8,128)} async-done(((f32[512,256]{1,0:T(8,128)}), f32[16,256]{1,0:T(8,128)}) %reduce-scatter.2.cloned.1.call-update) | async-done | bytes 16400 | tf_op jit(solution)/shard_map/reduce_scatter | solution.py:64
  (576 shorter events, 134.7 us)
Async XLA Ops:
  7.2 96.6 %all-gather.3.cloned.1.call-start = ((), (), s32[]{:S(2)}) async-start(), calls=%async_computation.5 | async-start | bytes 4718592 | tf_op jit(solution)/shard_map/all_gather | solution.py:39
  23.8 40.9 %copy-start.85 = (bf16[4096,1]{0,1:T(2,128)(2,1)S(1)}, bf16[4096,1]{0,1:T(2,128)(2,1)}, u32[]{:S(2)}) copy-start(bf16[4096,1]{0,1:T(2,128)(2,1)} %param.25) | copy-start | bytes 24580
  25.0 31.8 %all-to-all-start = ((bf16[16,128,256]{1,2,0:T(8,128)(2,1)}), bf16[16,128,256]{1,2,0:T(8,128)(2,1)S(1)}, u32[]{:S(2)}, u32[]{:S(2)}) async-start(bf16[16,128,256]{1,2,0:T(8,128)(2,1)} %broadcast_in_dim.637), calls=%async_computation | async-start | bytes 2097152 | tf_op jit(solution)/shard_map/all_to_all | solution.py:27
  58.1 54.6 %all-to-all-start.2 = ((bf16[16,128,256]{1,2,0:T(8,128)(2,1)}), bf16[16,128,256]{1,2,0:T(8,128)(2,1)}, u32[]{:S(2)}, u32[]{:S(2)}) async-start(bf16[16,128,256]{1,2,0:T(8,128)(2,1)} %broadcast_in_dim.644), calls=%async_computation.2 | async-start | bytes 2097152 | tf_op jit(solution)/shard_map/all_to_all | solution.py:27
  64.7 76.5 %all-gather.5.cloned.1.call-start = ((), (), s32[]{:S(2)}) async-start(), calls=%async_computation.6 | async-start | bytes 1769472 | tf_op jit(solution)/shard_map/all_gather | solution.py:39
  107.4 37.9 %copy-start = (f32[1,512,128]{2,1,0:T(8,128)S(1)}, f32[1,512,128]{2,1,0:T(8,128)}, u32[]{:S(2)}) copy-start(f32[1,512,128]{2,1,0:T(8,128)} %param.28) | copy-start | bytes 786436
  107.4 37.9 %copy-start.1 = (f32[1,128,512]{2,1,0:T(8,128)S(1)}, f32[1,128,512]{2,1,0:T(8,128)}, u32[]{:S(2)}) copy-start(f32[1,128,512]{2,1,0:T(8,128)} %param.27) | copy-start | bytes 786436
  181.1 24.4 %collective-permute-start = (f32[128,512]{1,0:T(8,128)S(1)}, f32[128,512]{1,0:T(8,128)}, u32[]{:S(2)}, u32[]{:S(2)}) collective-permute-start(f32[128,512]{1,0:T(8,128)S(1)} %get-tuple-element.7493), channel_id=1, source_target_pairs={{64,0},{128,64},{192,128},{256,192},{320,256},{384,320},{448,384},... | collective-permute-start | bytes 786440 | tf_op jit(solution)/shard_map/while/body/eval_jaxpr/ppermute | solution.py:58
  183.0 25.1 %collective-permute-start.1 = (f32[512,128]{1,0:T(8,128)S(1)}, f32[512,128]{1,0:T(8,128)S(1)}, u32[]{:S(2)}, u32[]{:S(2)}) collective-permute-start(f32[512,128]{1,0:T(8,128)S(1)} %get-tuple-element.7494), channel_id=1, source_target_pairs={{64,0},{128,64},{192,128},{256,192},{320,256},{384,320},{448,384},... | collective-permute-start | bytes 786440 | tf_op jit(solution)/shard_map/while/body/eval_jaxpr/ppermute | solution.py:58
  208.2 13.7 %collective-permute-start = (f32[128,512]{1,0:T(8,128)S(1)}, f32[128,512]{1,0:T(8,128)}, u32[]{:S(2)}, u32[]{:S(2)}) collective-permute-start(f32[128,512]{1,0:T(8,128)S(1)} %get-tuple-element.7493), channel_id=1, source_target_pairs={{64,0},{128,64},{192,128},{256,192},{320,256},{384,320},{448,384},... | collective-permute-start | bytes 786440 | tf_op jit(solution)/shard_map/while/body/eval_jaxpr/ppermute | solution.py:58
  210.2 14.5 %collective-permute-start.1 = (f32[512,128]{1,0:T(8,128)S(1)}, f32[512,128]{1,0:T(8,128)S(1)}, u32[]{:S(2)}, u32[]{:S(2)}) collective-permute-start(f32[512,128]{1,0:T(8,128)S(1)} %get-tuple-element.7494), channel_id=1, source_target_pairs={{64,0},{128,64},{192,128},{256,192},{320,256},{384,320},{448,384},... | collective-permute-start | bytes 786440 | tf_op jit(solution)/shard_map/while/body/eval_jaxpr/ppermute | solution.py:58
  224.7 19.0 %collective-permute-start = (f32[128,512]{1,0:T(8,128)S(1)}, f32[128,512]{1,0:T(8,128)}, u32[]{:S(2)}, u32[]{:S(2)}) collective-permute-start(f32[128,512]{1,0:T(8,128)S(1)} %get-tuple-element.7493), channel_id=1, source_target_pairs={{64,0},{128,64},{192,128},{256,192},{320,256},{384,320},{448,384},... | collective-permute-start | bytes 786440 | tf_op jit(solution)/shard_map/while/body/eval_jaxpr/ppermute | solution.py:58
  226.7 19.8 %collective-permute-start.1 = (f32[512,128]{1,0:T(8,128)S(1)}, f32[512,128]{1,0:T(8,128)S(1)}, u32[]{:S(2)}, u32[]{:S(2)}) collective-permute-start(f32[512,128]{1,0:T(8,128)S(1)} %get-tuple-element.7494), channel_id=1, source_target_pairs={{64,0},{128,64},{192,128},{256,192},{320,256},{384,320},{448,384},... | collective-permute-start | bytes 786440 | tf_op jit(solution)/shard_map/while/body/eval_jaxpr/ppermute | solution.py:58
  246.6 13.6 %collective-permute-start = (f32[128,512]{1,0:T(8,128)S(1)}, f32[128,512]{1,0:T(8,128)}, u32[]{:S(2)}, u32[]{:S(2)}) collective-permute-start(f32[128,512]{1,0:T(8,128)S(1)} %get-tuple-element.7493), channel_id=1, source_target_pairs={{64,0},{128,64},{192,128},{256,192},{320,256},{384,320},{448,384},... | collective-permute-start | bytes 786440 | tf_op jit(solution)/shard_map/while/body/eval_jaxpr/ppermute | solution.py:58
  248.5 14.4 %collective-permute-start.1 = (f32[512,128]{1,0:T(8,128)S(1)}, f32[512,128]{1,0:T(8,128)S(1)}, u32[]{:S(2)}, u32[]{:S(2)}) collective-permute-start(f32[512,128]{1,0:T(8,128)S(1)} %get-tuple-element.7494), channel_id=1, source_target_pairs={{64,0},{128,64},{192,128},{256,192},{320,256},{384,320},{448,384},... | collective-permute-start | bytes 786440 | tf_op jit(solution)/shard_map/while/body/eval_jaxpr/ppermute | solution.py:58
  263.0 18.9 %collective-permute-start = (f32[128,512]{1,0:T(8,128)S(1)}, f32[128,512]{1,0:T(8,128)}, u32[]{:S(2)}, u32[]{:S(2)}) collective-permute-start(f32[128,512]{1,0:T(8,128)S(1)} %get-tuple-element.7493), channel_id=1, source_target_pairs={{64,0},{128,64},{192,128},{256,192},{320,256},{384,320},{448,384},... | collective-permute-start | bytes 786440 | tf_op jit(solution)/shard_map/while/body/eval_jaxpr/ppermute | solution.py:58
  265.0 19.6 %collective-permute-start.1 = (f32[512,128]{1,0:T(8,128)S(1)}, f32[512,128]{1,0:T(8,128)S(1)}, u32[]{:S(2)}, u32[]{:S(2)}) collective-permute-start(f32[512,128]{1,0:T(8,128)S(1)} %get-tuple-element.7494), channel_id=1, source_target_pairs={{64,0},{128,64},{192,128},{256,192},{320,256},{384,320},{448,384},... | collective-permute-start | bytes 786440 | tf_op jit(solution)/shard_map/while/body/eval_jaxpr/ppermute | solution.py:58
  284.7 176.5 %collective-permute-start = (f32[128,512]{1,0:T(8,128)S(1)}, f32[128,512]{1,0:T(8,128)}, u32[]{:S(2)}, u32[]{:S(2)}) collective-permute-start(f32[128,512]{1,0:T(8,128)S(1)} %get-tuple-element.7493), channel_id=1, source_target_pairs={{64,0},{128,64},{192,128},{256,192},{320,256},{384,320},{448,384},... | collective-permute-start | bytes 786440 | tf_op jit(solution)/shard_map/while/body/eval_jaxpr/ppermute | solution.py:58
  286.6 177.2 %collective-permute-start.1 = (f32[512,128]{1,0:T(8,128)S(1)}, f32[512,128]{1,0:T(8,128)S(1)}, u32[]{:S(2)}, u32[]{:S(2)}) collective-permute-start(f32[512,128]{1,0:T(8,128)S(1)} %get-tuple-element.7494), channel_id=1, source_target_pairs={{64,0},{128,64},{192,128},{256,192},{320,256},{384,320},{448,384},... | collective-permute-start | bytes 786440 | tf_op jit(solution)/shard_map/while/body/eval_jaxpr/ppermute | solution.py:58
  491.2 8.7 %collective-permute-start = (f32[128,512]{1,0:T(8,128)S(1)}, f32[128,512]{1,0:T(8,128)}, u32[]{:S(2)}, u32[]{:S(2)}) collective-permute-start(f32[128,512]{1,0:T(8,128)S(1)} %get-tuple-element.7493), channel_id=1, source_target_pairs={{64,0},{128,64},{192,128},{256,192},{320,256},{384,320},{448,384},... | collective-permute-start | bytes 786440 | tf_op jit(solution)/shard_map/while/body/eval_jaxpr/ppermute | solution.py:58
  493.1 9.5 %collective-permute-start.1 = (f32[512,128]{1,0:T(8,128)S(1)}, f32[512,128]{1,0:T(8,128)S(1)}, u32[]{:S(2)}, u32[]{:S(2)}) collective-permute-start(f32[512,128]{1,0:T(8,128)S(1)} %get-tuple-element.7494), channel_id=1, source_target_pairs={{64,0},{128,64},{192,128},{256,192},{320,256},{384,320},{448,384},... | collective-permute-start | bytes 786440 | tf_op jit(solution)/shard_map/while/body/eval_jaxpr/ppermute | solution.py:58
  506.4 22.8 %all-to-all-start.3 = ((bf16[16,128,256]{2,1,0:T(8,128)(2,1)}), bf16[16,128,256]{2,1,0:T(8,128)(2,1)S(1)}, u32[]{:S(2)}, u32[]{:S(2)}) async-start(bf16[16,128,256]{2,1,0:T(8,128)(2,1)} %bitcast.946), calls=%async_computation.3 | async-start | bytes 2097152 | tf_op jit(solution)/shard_map/all_to_all | solution.py:51
  529.2 138.6 %all-to-all-start.1 = ((bf16[16,128,256]{2,1,0:T(8,128)(2,1)}), bf16[16,128,256]{2,1,0:T(8,128)(2,1)S(1)}, u32[]{:S(2)}, u32[]{:S(2)}) async-start(bf16[16,128,256]{2,1,0:T(8,128)(2,1)} %bitcast.948), calls=%async_computation.1 | async-start | bytes 2097152 | tf_op jit(solution)/shard_map/all_to_all | solution.py:51
  533.7 132.0 %reduce-scatter.2.cloned.1.call-start = ((), (), s32[]{:S(2)}) async-start(), calls=%async_computation.7 | async-start | bytes 540672 | tf_op jit(solution)/shard_map/reduce_scatter | solution.py:64
  (126 other events, 710.4 us)
Sparse Core Ops, SparseCore 0:
  22.9 80.7 all-gather.2
  108.2 32.8 all-gather.4
  538.8 126.8 reduce-scatter.1
where the time goes:
time: 680 us; the launch traced here: 675 us
  waiting for transfers between devices  493 us (72%)
  starting transfers between devices  53.3 us (8%)
  local copies, waits for them, and re-layouts  39 us (6%)
  matrix products  36.5 us (5%)
  other arithmetic  22.6 us (3%)
  between operations  14.4 us (2%)
  blocking collectives  13.7 us (2%)
    ppermute x14, waiting for transfers between devices, shifted(): return lax.ppermute(array, axis, pairs)  260 us
    reduce_scatter x1, waiting for transfers between devices, side_by_side(): out = lax.psum_scatter(both, axis, scatter_dimension=dim, tiled=True)  131 us
    all_gather x2, waiting for transfers between devices, in_one_piece(): out = lax.all_gather(both, axis, axis=dim, tiled=True)  65.1 us
    ppermute x14, starting transfers between devices, shifted(): return lax.ppermute(array, axis, pairs)  26.9 us
    all_to_all x2, waiting for transfers between devices, from_everyone(): return lax.all_to_all(copies, axis, split_axis=0, concat_axis=0, tiled=True)  23.5 us
    dot_general x34, matrix products, float_dims(): return lax.dot_general(left, right, dims)  15.8 us
    all_to_all x2, starting transfers between devices, from_everyone(): return lax.all_to_all(copies, axis, split_axis=0, concat_axis=0, tiled=True)  14.8 us
    all_gather x1, blocking collectives, in_one_piece(): out = lax.all_gather(both, axis, axis=dim, tiled=True)  13.7 us
  transfers between devices with their start and end apart: 21, of which 19 were waited for; matrix products, arithmetic and copies ran while one was open for 4% of the time, Pallas kernels for 0%

commit v1 on v0

v1 whole, which is shorter than its diff:
```python
import math

import jax
import jax.numpy as jnp
from jax import lax
from jax.experimental import pallas as pl
from jax.experimental.pallas import tpu as pltpu
from jax.sharding import PartitionSpec as P

MB = 64
HD = 128
BF16 = jnp.bfloat16
F32 = jnp.float32
MESH = pl.DeviceIdType.MESH
EPSILON = 1e-06
BASE_RATE = 0.1
GELU_SCALE = 0.7978845608028654
GELU_CUBIC = 0.044715
CONTRACT_LAST = (((1,), (1,)), ((), ()))
CONTRACT_FIRST = (((0,), (0,)), ((), ()))


def joined_along(parts, dim):
    parts = jnp.moveaxis(parts, 0, dim)
    lengths = parts.shape
    return parts.reshape(*lengths[:dim], lengths[dim] * lengths[dim + 1], *lengths[dim + 2 :])


def from_everyone(array, axis):
    copies = jnp.broadcast_to(array, (lax.axis_size(axis), *array.shape))
    return lax.all_to_all(copies, axis, split_axis=0, concat_axis=0, tiled=True)


def gather_directly(array, axis, dim):
    return joined_along(from_everyone(array, axis), dim)


def in_one_piece(arrays, axis, dim, along):
    widths = [math.prod(a.shape[along:]) for a in arrays]
    both = jnp.concatenate(
        [a.reshape(*a.shape[:along], w) for a, w in zip(arrays, widths)], axis=along
    )
    out = lax.all_gather(both, axis, axis=dim, tiled=True)
    parts = jnp.split(out, [sum(widths[:k]) for k in range(1, len(widths))], axis=along)
    return tuple((b.reshape(*out.shape[:along], *a.shape[along:]) for a, b in zip(arrays, parts)))


def in_blocks(array, dim, peers):
    before, after = (array.shape[:dim], array.shape[dim + 1 :])
    return jnp.moveaxis(array.reshape(*before, peers, -1, *after), dim, 0)


def summed_on_arrival(array, axis, dim):
    peers = lax.axis_size(axis)
    parts = lax.all_to_all(in_blocks(array, dim, peers), axis, 0, 0, tiled=True)
    return jnp.sum(parts.astype(jnp.float32), axis=0)


def matmul(left, right):
    return jnp.dot(left.astype(BF16), right.astype(BF16), preferred_element_type=F32)


def matmul_last(left, right):
    return lax.dot_general(left.astype(BF16), right.astype(BF16), CONTRACT_LAST, preferred_element_type=F32)


def matmul_first(left, right):
    return lax.dot_general(left.astype(BF16), right.astype(BF16), CONTRACT_FIRST, preferred_element_type=F32)


def row_mean(rows):
    return jnp.mean(rows, axis=-1, keepdims=True)


def row_sum(rows):
    return jnp.sum(rows, axis=-1, keepdims=True)


def spread(rates):
    return jnp.concatenate([rates] * 4, axis=1)


def gelu_parts(v, order):
    square = v * v
    bend = jnp.tanh(GELU_SCALE * (v + GELU_CUBIC * square * v))
    tilt = GELU_SCALE * (1.0 + 3.0 * GELU_CUBIC * square)
    flat = 1.0 - bend * bend
    half = 0.5 * v
    value = half * (1.0 + bend)
    slope = 0.5 * (1.0 + bend) + half * flat * tilt
    if order == 1:
        return value, slope
    curve = flat * (tilt + half * (6.0 * GELU_SCALE * GELU_CUBIC) * v - v * bend * tilt * tilt)
    return value, slope, curve


def norm_rows(rows):
    centred = rows - row_mean(rows)
    inv_scale = lax.rsqrt(row_mean(centred * centred) + EPSILON)
    return centred * inv_scale, inv_scale


def inner_kernel(
    q_ref, k_ref, t_ref, e_ref, chunk_ref, dt_ref, w1_ref, w2_ref,
    out_ref, dproj_ref, dlogit_ref, dw1_ref, dw2_ref,
    chunks, s1, s2, in1, in2, snd1, snd2, w1b, w2b,
    sv_wide, sv_x2, sv_narrow, sv_kt, sv_x2t, sv_eg1, b_w1, b_w2,
    chunk_send, chunk_recv, hop_send, hop_recv,
):
    place = lax.axis_index("seq")
    count = lax.axis_size("seq")
    barrier = pltpu.get_barrier_semaphore()

    def greet(step, carry):
        pl.semaphore_signal(
            barrier, inc=1, device_id={"seq": lax.rem(place + step, count)}, device_id_type=MESH
        )
        return carry

    lax.fori_loop(1, count, greet, 0)
    pl.semaphore_wait(barrier, count - 1)

    def chunk_copy(source, target):
        return pltpu.make_async_remote_copy(
            src_ref=chunk_ref,
            dst_ref=chunks.at[source],
            send_sem=chunk_send.at[target],
            recv_sem=chunk_recv.at[source],
            device_id={"seq": target},
            device_id_type=MESH,
        )

    def send_chunk(step, carry):
        chunk_copy(place, count - 1 - step).start()
        return carry

    lax.fori_loop(0, count - 1 - place, send_chunk, 0)

    s1[...] = w1_ref[...]
    s2[...] = w2_ref[...]

    def replay_block(k, t, e):
        first, second = s1[...].astype(BF16), s2[...].astype(BF16)
        x2, slope = gelu_parts(matmul(k, first), 1)
        n, s = norm_rows(matmul(x2, second))
        r = n - t
        g2 = s * (r - row_mean(r) - n * row_mean(r * n))
        g1 = matmul_last(g2, second) * slope
        s1[...] = s1[...] - matmul_first(k, spread(e) * g1)
        s2[...] = s2[...] - matmul_first(x2, e * g2)

    def replay_turn(turn, carry):
        chunk_copy(turn, place).wait_recv()
        for half in range(2):
            rows = chunks[turn, half * MB : (half + 1) * MB, :]
            replay_block(
                rows[:, :HD], rows[:, HD : 2 * HD].astype(F32), rows[:, 2 * HD :].astype(F32)
            )
        return carry

    lax.fori_loop(0, place, replay_turn, 0)

    place_row = lax.broadcasted_iota(jnp.int32, (MB, MB), 0)
    place_col = lax.broadcasted_iota(jnp.int32, (MB, MB), 1)
    for block in range(2):
        span = slice(block * MB, (block + 1) * MB)
        q, k, t, e = q_ref[span, :], k_ref[span, :], t_ref[span, :], e_ref[span, :]
        first, second = s1[...].astype(BF16), s2[...].astype(BF16)
        w1b[block] = first
        w2b[block] = second
        x2, slope, curve = gelu_parts(matmul(k, first), 2)
        n, s = norm_rows(matmul(x2, second))
        r = n - t
        cross = row_mean(r * n)
        h = r - row_mean(r) - n * cross
        g2 = s * h
        m = matmul_last(g2, second)
        g1 = m * slope
        e_wide = spread(e)
        eg1 = e_wide * g1
        eg2 = e * g2
        kt = jnp.transpose(k)
        x2t = jnp.transpose(x2)
        s1[...] = s1[...] - matmul(kt, eg1)
        s2[...] = s2[...] - matmul(x2t, eg2)

        e_row = jnp.transpose(e)[:MB, :]
        causal = jnp.where(place_col <= place_row, e_row, 0.0)
        raw1 = matmul_last(q, k)
        a1 = raw1 * causal
        zq = matmul(q, first) - matmul(a1, g1)
        xq, slope_q = gelu_parts(zq, 1)
        raw2 = matmul_last(xq, x2)
        a2 = raw2 * causal
        nq, sq = norm_rows(matmul(xq, second) - matmul(a2, g2))
        out_ref[span, :] = (q + nq).astype(BF16)
        do = dt_ref[span, :]
        dyq = sq * (do - row_mean(do) - nq * row_mean(do * nq))
        da2 = -matmul_last(dyq, g2)
        ds2 = da2 * causal
        dxq = matmul_last(dyq, second) + matmul(ds2, x2)
        dzq = dxq * slope_q
        da1 = -matmul_last(dzq, g1)
        ds1 = da1 * causal
        kept = jnp.where(place_col <= place_row, da2 * raw2 + da1 * raw1, 0.0)
        de_col = row_sum(jnp.transpose(kept))
        dproj_ref[span, :HD] = (do + matmul_last(dzq, first) + matmul(ds1, k)).astype(BF16)
        b_w1[block] = matmul_first(q, dzq)
        b_w2[block] = matmul_first(xq, dyq)
        sv_wide[block, 0] = -matmul_first(a1, dzq)
        sv_wide[block, 1] = matmul_first(ds2, xq)
        sv_wide[block, 2] = slope
        sv_wide[block, 3] = curve
        sv_wide[block, 4] = m
        sv_x2[block] = x2.astype(BF16)
        sv_eg1[block] = eg1.astype(BF16)
        sv_kt[block] = kt.astype(BF16)
        sv_x2t[block] = x2t.astype(BF16)
        sv_narrow[block, 0] = -matmul_first(a2, dyq)
        sv_narrow[block, 1] = matmul_first(ds1, q)
        sv_narrow[block, 2] = jnp.broadcast_to(de_col, (MB, HD))
        sv_narrow[block, 3] = n
        sv_narrow[block, 4] = r
        sv_narrow[block, 5] = h
        sv_narrow[block, 6] = g2
        sv_narrow[block, 7] = jnp.broadcast_to(s, (MB, HD))
        sv_narrow[block, 8] = jnp.broadcast_to(cross, (MB, HD))
        sv_narrow[block, 9] = eg2

    def hop(target, which):
        return pltpu.make_async_remote_copy(
            src_ref=(snd1, snd2)[which],
            dst_ref=(in1, in2)[which],
            send_sem=hop_send.at[which],
            recv_sem=hop_recv.at[which],
            device_id={"seq": target},
            device_id_type=MESH,
        )

    @pl.when(place == count - 1)
    def _():
        in1[...] = jnp.zeros_like(in1)
        in2[...] = jnp.zeros_like(in2)

    @pl.when(place < count - 1)
    def _():
        hop(0, 0).wait_recv()
        hop(0, 1).wait_recv()

    for block in (1, 0):
        span = slice(block * MB, (block + 1) * MB)
        if block == 1:
            d1b, d2b = in1[...], in2[...]
            d1, d2 = d1b.astype(F32), d2b.astype(F32)
        else:
            d1, d2 = dw1_ref[...], dw2_ref[...]
            d1b, d2b = d1.astype(BF16), d2.astype(BF16)
        k, e = k_ref[span, :], e_ref[span, :]
        first, second = w1b[block], w2b[block]
        b_g1, b_x2, slope, curve, m = (sv_wide[block, i] for i in range(5))
        b_g2, b_k, b_e, n, r, h, g2, s, cross, eg2 = (sv_narrow[block, i] for i in range(10))
        x2 = sv_x2[block]
        p1 = matmul(k, d1b)
        p2 = matmul(x2, d2b)
        dg1 = b_g1 - spread(e) * p1
        dm = dg1 * slope
        dmb = dm.astype(BF16)
        dg2 = b_g2 - e * p2 + matmul(dmb, second)
        dh = s * dg2
        mean_n = row_mean(dh * n)
        dr = dh - row_mean(dh) - n * mean_n
        dn = dr - cross * dh - r * mean_n
        dy = s * (dn - row_mean(dn) - n * row_mean(dn * n)) - n * (row_mean(dg2 * h) * s * s)
        dyb = dy.astype(BF16)
        dx2 = b_x2 - matmul_last(eg2, d2b) + matmul_last(dyb, second)
        dz1 = dx2 * slope + dg1 * m * curve
        dz1b = dz1.astype(BF16)
        d2 = d2 + b_w2[block] + matmul_first(dmb, g2) + matmul(sv_x2t[block], dyb)
        d1 = d1 + b_w1[block] + matmul(sv_kt[block], dz1b)
        dw1_ref[...] = d1
        dw2_ref[...] = d2
        if block == 0:
            snd1[...] = d1.astype(BF16)
            snd2[...] = d2.astype(BF16)

            @pl.when(place > 0)
            def _():
                hop(place - 1, 0).start()
                hop(place - 1, 1).start()

        dk = b_k - matmul_last(sv_eg1[block], d1b) + dr + matmul_last(dz1b, first)
        de = b_e - row_sum(p1 * m * slope) - row_sum(p2 * g2)
        dproj_ref[span, HD : 2 * HD] = dk.astype(BF16)
        dproj_ref[span, 2 * HD :] = (-dr).astype(BF16)
        dlogit_ref[span, :] = de * e * (1.0 - e * (HD / BASE_RATE))

    @pl.when(place > 0)
    def _():
        hop(place - 1, 0).wait_send()
        hop(place - 1, 1).wait_send()

    def sent_chunk(step, carry):
        chunk_copy(place, count - 1 - step).wait_send()
        return carry

    lax.fori_loop(0, count - 1 - place, sent_chunk, 0)


def inner_layer(q, k, t, e, chunk, d_ttt, w_first, w_second):
    rows = q.shape[0]
    peers = lax.axis_size("seq")
    inner = w_first.shape[1]
    vmem = pl.BlockSpec(memory_space=pltpu.VMEM)
    return pl.pallas_call(
        inner_kernel,
        out_shape=(
            jax.ShapeDtypeStruct((rows, HD), BF16),
            jax.ShapeDtypeStruct((rows, 3 * HD), BF16),
            jax.ShapeDtypeStruct((rows, HD), F32),
            jax.ShapeDtypeStruct((HD, inner), F32),
            jax.ShapeDtypeStruct((inner, HD), F32),
        ),
        in_specs=[vmem] * 8,
        out_specs=(vmem,) * 5,
        scratch_shapes=[
            pltpu.VMEM((peers, rows, 3 * HD), BF16),
            pltpu.VMEM((HD, inner), F32),
            pltpu.VMEM((inner, HD), F32),
            pltpu.VMEM((HD, inner), BF16),
            pltpu.VMEM((inner, HD), BF16),
            pltpu.VMEM((HD, inner), BF16),
            pltpu.VMEM((inner, HD), BF16),
            pltpu.VMEM((2, HD, inner), BF16),
            pltpu.VMEM((2, inner, HD), BF16),
            pltpu.VMEM((2, 5, MB, inner), F32),
            pltpu.VMEM((2, MB, inner), BF16),
            pltpu.VMEM((2, 10, MB, HD), F32),
            pltpu.VMEM((2, HD, MB), BF16),
            pltpu.VMEM((2, inner, MB), BF16),
            pltpu.VMEM((2, MB, inner), BF16),
            pltpu.VMEM((2, HD, inner), F32),
            pltpu.VMEM((2, inner, HD), F32),
            pltpu.SemaphoreType.DMA((peers,)),
            pltpu.SemaphoreType.DMA((peers,)),
            pltpu.SemaphoreType.DMA((2,)),
            pltpu.SemaphoreType.DMA((2,)),
        ],
        compiler_params=pltpu.CompilerParams(collective_id=0, has_side_effects=True),
        name="inner_layer",
    )(q, k, t, e, chunk, d_ttt, w_first, w_second)


def gradient_shares(first, second):
    peers, groups = lax.axis_size("seq"), lax.axis_size("dp")
    both = jnp.concatenate([first.transpose(1, 0), second], axis=1)
    width = both.shape[1]
    parts = both.reshape(peers, groups, -1, width).transpose(1, 0, 2, 3)
    summed = jnp.sum(lax.all_to_all(parts, "dp", 0, 0, tiled=True), axis=0)
    own = lax.all_to_all(summed, "seq", 0, 0, tiled=True)[0]
    return own[:, :HD].transpose(1, 0)[None], own[:, HD:][None]


def body(tokens, w_qkv, w_lr, w_out, w1_init, w2_init, d_out):
    head_width = w_qkv.shape[2]
    features = gather_directly(tokens[0], "head", 1)
    part_qkv, part_out = in_one_piece((w_qkv, w_out), "dp", 0, 1)
    wide_qkv, wide_out = in_one_piece((part_qkv, part_out), "seq", 0, 1)
    full_depth = wide_qkv.shape[0]
    qkv_matrix = wide_qkv.reshape(full_depth, 3 * head_width)
    projected = jnp.dot(features, qkv_matrix, preferred_element_type=F32)
    rate_logit = jnp.dot(features, w_lr, preferred_element_type=F32)
    queries = projected[:, :head_width]
    key_rows = projected[:, head_width : 2 * head_width]
    target = projected[:, 2 * head_width :] - key_rows
    rates = jnp.broadcast_to(BASE_RATE * jax.nn.sigmoid(rate_logit) / head_width, target.shape)
    chunk = jnp.concatenate([key_rows, target, rates], axis=1).astype(BF16)
    d_full = gather_directly(d_out[0], "head", 1)
    d_ttt = jnp.dot(d_full, wide_out, preferred_element_type=F32)
    ttt_out, d_proj, d_logit, d_first, d_second = inner_layer(
        queries, key_rows, target, rates, chunk, d_ttt, w1_init[0], w2_init[0]
    )
    out_term = lax.dot_general(ttt_out, wide_out, CONTRACT_LAST, preferred_element_type=F32)
    out = summed_on_arrival(out_term.astype(BF16), "head", 1).astype(BF16)[None]
    grad_term = lax.dot_general(d_proj, qkv_matrix, CONTRACT_LAST, preferred_element_type=F32)
    grad_term = grad_term + d_logit[:, :1] * w_lr[:, 0].astype(F32)[None, :]
    d_tokens = summed_on_arrival(grad_term.astype(BF16), "head", 1).astype(BF16)[None]
    share_first, share_second = gradient_shares(d_first, d_second)
    return (out, d_tokens, share_first, share_second)


def solution(mesh):
    placed = (
        P("dp", "seq", "head"),
        P(("seq", "dp"), None, "head"),
        P(None, "head"),
        P(("seq", "dp"), "head"),
        P("head", None, None),
        P("head", None, None),
        P("dp", "seq", "head"),
    )
    return jax.shard_map(
        body,
        mesh=mesh,
        in_specs=placed,
        out_specs=(
            P("dp", "seq", "head"),
            P("dp", "seq", "head"),
            P("head", None, ("seq", "dp")),
            P("head", ("seq", "dp"), None),
        ),
        check_vma=False,
    )
```

time: 680 us -> 285 us (0.42)
  waiting for transfers between devices: 493 us -> 120 us
  Pallas kernels: 0 us -> 72 us
  local copies, waits for them, and re-layouts: 39 us -> 10.9 us
  matrix products: 36.5 us -> 9.77 us
  other arithmetic: 22.6 us -> 4.63 us
  starting transfers between devices: 53.3 us -> 38.8 us
    ppermute x14 -> x0, waiting for transfers between devices: 260 us -> none  [shifted(): return lax.ppermute(array, axis, pairs)]
    reduce_scatter x1 -> x0, waiting for transfers between devices: 131 us -> none  [side_by_side(): out = lax.psum_scatter(both, axis, scatter_dimension=dim, tiled=True)]
    pallas_call x0 -> x1, Pallas kernels: none -> 72 us  [inner_layer(): pl.pallas_call(inner_kernel, out_shape=(jax.ShapeDtypeStruct((rows, HD),...]
    all_to_all x2, waiting for transfers between devices: 13 us -> 46 us  [summed_on_arrival(): parts = lax.all_to_all(in_blocks(array, dim, peers), axis, 0, 0, tiled=True)]
    ppermute x14 -> x0, starting transfers between devices: 26.9 us -> none  [shifted(): return lax.ppermute(array, axis, pairs)]
    dot_general x77 -> x3, matrix products: 32.3 us -> 5.49 us  [the longest x1 2.88 us: body(): projected = jnp.dot(features, qkv_matrix, preferred_element_type=F32)]
    all_gather x2 -> x1, waiting for transfers between devices: 65.1 us -> 39 us  [in_one_piece(): out = lax.all_gather(both, axis, axis=dim, tiled=True)]
    all_to_all x0 -> x2, waiting for transfers between devices: none -> 11.1 us  [the longest x1 6.77 us: gradient_shares(): summed = jnp.sum(lax.all_to_all(parts, 'dp', 0, 0, tiled=True), axis=0)]
  transfers between devices with their start and end apart: 21 -> 7, of which waited for: 19 -> 6; matrix products, arithmetic and copies ran while one was open for 4% -> 6% of each run, Pallas kernels for 0% -> 0%
where the time goes in v1:
time: 285 us; the launch traced here: 284 us
  waiting for transfers between devices  120 us (42%)
  Pallas kernels  72 us (25%)
  starting transfers between devices  38.8 us (14%)
  between operations  14.2 us (5%)
  blocking collectives  13.7 us (5%)
  local copies, waits for them, and re-layouts  10.9 us (4%)
  matrix products  9.77 us (3%)
  other arithmetic  4.63 us (2%)
    pallas_call x1, Pallas kernels, inner_layer(): pl.pallas_call(inner_kernel, out_shape=(jax.ShapeDtypeStruct((rows, HD),...  72 us
    all_to_all x2, waiting for transfers between devices, summed_on_arrival(): parts = lax.all_to_all(in_blocks(array, dim, peers), axis, 0, 0, tiled=True)  46 us
    all_gather x1, waiting for transfers between devices, in_one_piece(): out = lax.all_gather(both, axis, axis=dim, tiled=True)  39 us
    all_to_all x2, waiting for transfers between devices, from_everyone(): return lax.all_to_all(copies, axis, split_axis=0, concat_axis=0, tiled=True)  23.5 us
    all_to_all x2, starting transfers between devices, from_everyone(): return lax.all_to_all(copies, axis, split_axis=0, concat_axis=0, tiled=True)  14.8 us
    all_gather x1, blocking collectives, in_one_piece(): out = lax.all_gather(both, axis, axis=dim, tiled=True)  13.7 us
    all_to_all x2, starting transfers between devices, summed_on_arrival(): parts = lax.all_to_all(in_blocks(array, dim, peers), axis, 0, 0, tiled=True)  13.3 us
    all_to_all x1, starting transfers between devices, gradient_shares(): own = lax.all_to_all(summed, 'seq', 0, 0, tiled=True)[0]  6.85 us
  transfers between devices with their start and end apart: 7, of which 6 were waited for; matrix products, arithmetic and copies ran while one was open for 6% of the time, Pallas kernels for 0%

profile of v1, /device:TPU:1, one launch (start us, length us, event | category | flops | bytes accessed | tf_op | source)
XLA Modules:
  0.0 283.5 jit_solution(2146514292081082477)
XLA Ops:
  8.1 1.0 copy.21
  9.1 13.7 %all_gather.6 = bf16[512,512]{0,1:T(8,128)(2,1)} all-gather(bf16[128,512]{0,1:T(8,128)(2,1)S(1)} %pad_maximum_fusion.1), channel_id=1, replica_groups=mesh['seq'=8,'head'=16,'dp'=4] {'dp'}, dimensions={0}, use_global_device_ids=true | all-gather | bytes 655360 | tf_op jit(solution)/shard_map/all_gather | solution.py:43
  23.8 1.2 broadcast_in_dim.26
  25.0 8.2 %all-to-all-start = ((bf16[16,128,256]{1,2,0:T(8,128)(2,1)}), bf16[16,128,256]{1,2,0:T(8,128)(2,1)S(1)}, u32[]{:S(2)}, u32[]{:S(2)}) async-start(bf16[16,128,256]{1,2,0:T(8,128)(2,1)} %broadcast_in_dim.26), calls=%async_computation | async-start | bytes 2097152 | tf_op jit(solution)/shard_map/all_to_all | solution.py:31
  33.3 23.5 %all-to-all-done = bf16[16,128,256]{1,2,0:T(8,128)(2,1)S(1)} async-done(((bf16[16,128,256]{1,2,0:T(8,128)(2,1)}), bf16[16,128,256]{1,2,0:T(8,128)(2,1)S(1)}, u32[]{:S(2)}, u32[]{:S(2)}) %all-to-all-start) | async-done | bytes 1048608 | tf_op jit(solution)/shard_map/all_to_all | solution.py:31
  56.8 1.2 broadcast_in_dim.29
  57.9 6.5 %all-to-all-start.1 = ((bf16[16,128,256]{1,2,0:T(8,128)(2,1)}), bf16[16,128,256]{1,2,0:T(8,128)(2,1)S(1)}, u32[]{:S(2)}, u32[]{:S(2)}) async-start(bf16[16,128,256]{1,2,0:T(8,128)(2,1)} %broadcast_in_dim.29), calls=%async_computation.1 | async-start | bytes 2097152 | tf_op jit(solution)/shard_map/all_to_all | solution.py:31
  64.7 39.0 %all-gather.2.cloned.1.call-done = bf16[4096,512]{0,1:T(8,128)(2,1)} async-done(((bf16[512,512]{0,1:T(8,128)(2,1)}), bf16[4096,512]{0,1:T(8,128)(2,1)}) %all-gather.2.cloned.1.call-update) | async-done | bytes 4194320 | tf_op jit(solution)/shard_map/all_gather | solution.py:43
  103.8 2.9 %fusion.4 = f32[128,384]{1,0:T(8,128)S(1)} fusion(bf16[128,4096]{0,1:T(8,128)(2,1)S(1)} %bitcast.64, bf16[4096,512]{0,1:T(8,128)(2,1)} %all-gather.2.cloned.1.call-done), kind=kOutput, calls=%fused_computation.6 | convolution fusion | flops 402653184 | bytes 4390912 | tf_op jit(solution)/shard_map/dot_general | solution.py:370
  108.1 2.4 convolution_bitcast_fusion.dt_ref
  111.2 72.0 %inner_layer.1 = (bf16[128,128]{1,0:T(8,128)(2,1)}, bf16[128,384]{1,0:T(8,128)(2,1)}, f32[128,128]{1,0:T(8,128)}, f32[128,512]{1,0:T(8,128)}, f32[512,128]{1,0:T(8,128)}) custom-call(f32[128,128]{1,0:T(8,128)} %get-tuple-element.17.q_ref, f32[128,128]{1,0:T(8,128)} %get-tuple-element.16.k_ref, f32[128,128]{1,0:T(8,128)} %get-tuple-element.15.t_ref, ...), custom_call_target="tpu_custom_call" | custom-call | tf_op jit(solution)/shard_map/inner_layer/pallas_call | solution.py:314
  183.1 1.1 copy.29
  186.1 3.8 %all-to-all-start.4 = ((f32[4,8,16,256]{3,2,1,0:T(8,128)}), f32[4,8,16,256]{3,2,1,0:T(8,128)S(1)}, u32[]{:S(2)}, u32[]{:S(2)}) async-start(f32[4,8,16,256]{3,2,1,0:T(8,128)} %bitcast.61), calls=%async_computation.4 | async-start | bytes 1048576 | tf_op jit(solution)/shard_map/all_to_all | solution.py:358
  190.1 6.8 %all-to-all-done.4 = f32[4,8,16,256]{3,2,1,0:T(8,128)S(1)} async-done(((f32[4,8,16,256]{3,2,1,0:T(8,128)}), f32[4,8,16,256]{3,2,1,0:T(8,128)S(1)}, u32[]{:S(2)}, u32[]{:S(2)}) %all-to-all-start.4) | async-done | bytes 524320 | tf_op jit(solution)/shard_map/all_to_all | solution.py:358
  197.6 6.9 %all-to-all-start.5 = ((f32[8,16,256]{2,1,0:T(8,128)}), f32[8,16,256]{2,1,0:T(8,128)S(1)}, u32[]{:S(2)}, u32[]{:S(2)}) async-start(f32[8,16,256]{2,1,0:T(8,128)} %reduce_sum.35), calls=%async_computation.5 | async-start | bytes 262144 | tf_op jit(solution)/shard_map/all_to_all | solution.py:359
  204.4 2.6 fusion
  207.1 1.1 copy.38
  208.2 4.3 %all-to-all-done.5 = f32[8,16,256]{2,1,0:T(8,128)S(1)} async-done(((f32[8,16,256]{2,1,0:T(8,128)}), f32[8,16,256]{2,1,0:T(8,128)S(1)}, u32[]{:S(2)}, u32[]{:S(2)}) %all-to-all-start.5) | async-done | bytes 131104 | tf_op jit(solution)/shard_map/all_to_all | solution.py:359
  212.4 6.2 %all-to-all-start.3 = ((bf16[16,128,256]{2,1,0:T(8,128)(2,1)}), bf16[16,128,256]{2,1,0:T(8,128)(2,1)S(1)}, u32[]{:S(2)}, u32[]{:S(2)}) async-start(bf16[16,128,256]{2,1,0:T(8,128)(2,1)} %bitcast.58), calls=%async_computation.3 | async-start | bytes 2097152 | tf_op jit(solution)/shard_map/all_to_all | solution.py:55
  218.7 1.6 convolution_convert_fusion
  220.3 1.1 copy.39
  221.4 21.8 %all-to-all-done.3 = bf16[16,128,256]{2,1,0:T(8,128)(2,1)S(1)} async-done(((bf16[16,128,256]{2,1,0:T(8,128)(2,1)}), bf16[16,128,256]{2,1,0:T(8,128)(2,1)S(1)}, u32[]{:S(2)}, u32[]{:S(2)}) %all-to-all-start.3) | async-done | bytes 1048608 | tf_op jit(solution)/shard_map/all_to_all | solution.py:55
  243.2 7.1 %all-to-all-start.2 = ((bf16[16,128,256]{2,1,0:T(8,128)(2,1)}), bf16[16,128,256]{2,1,0:T(8,128)(2,1)S(1)}, u32[]{:S(2)}, u32[]{:S(2)}) async-start(bf16[16,128,256]{2,1,0:T(8,128)(2,1)} %bitcast.60), calls=%async_computation.2 | async-start | bytes 2097152 | tf_op jit(solution)/shard_map/all_to_all | solution.py:55
  251.7 24.2 %all-to-all-done.2 = bf16[16,128,256]{2,1,0:T(8,128)(2,1)S(1)} async-done(((bf16[16,128,256]{2,1,0:T(8,128)(2,1)}), bf16[16,128,256]{2,1,0:T(8,128)(2,1)S(1)}, u32[]{:S(2)}, u32[]{:S(2)}) %all-to-all-start.2) | async-done | bytes 1048608 | tf_op jit(solution)/shard_map/all_to_all | solution.py:55
  (33 shorter events, 9.2 us)
Async XLA Ops:
  7.2 26.0 %copy-start.1 = (bf16[1,128,256]{2,1,0:T(8,128)(2,1)S(1)}, bf16[1,128,256]{2,1,0:T(8,128)(2,1)}, u32[]{:S(2)}) copy-start(bf16[1,128,256]{2,1,0:T(8,128)(2,1)} %param.13) | copy-start | bytes 196612
  7.2 96.6 %all-gather.2.cloned.1.call-start = ((), (), s32[]{:S(2)}) async-start(), calls=%async_computation.6 | async-start | bytes 4718592 | tf_op jit(solution)/shard_map/all_gather | solution.py:43
  23.8 40.7 %copy-start = (bf16[4096,1]{0,1:T(2,128)(2,1)S(1)}, bf16[4096,1]{0,1:T(2,128)(2,1)}, u32[]{:S(2)}) copy-start(bf16[4096,1]{0,1:T(2,128)(2,1)} %param.9) | copy-start | bytes 24580
  25.0 31.8 %all-to-all-start = ((bf16[16,128,256]{1,2,0:T(8,128)(2,1)}), bf16[16,128,256]{1,2,0:T(8,128)(2,1)S(1)}, u32[]{:S(2)}, u32[]{:S(2)}) async-start(bf16[16,128,256]{1,2,0:T(8,128)(2,1)} %broadcast_in_dim.26), calls=%async_computation | async-start | bytes 2097152 | tf_op jit(solution)/shard_map/all_to_all | solution.py:31
  57.9 50.1 %all-to-all-start.1 = ((bf16[16,128,256]{1,2,0:T(8,128)(2,1)}), bf16[16,128,256]{1,2,0:T(8,128)(2,1)S(1)}, u32[]{:S(2)}, u32[]{:S(2)}) async-start(bf16[16,128,256]{1,2,0:T(8,128)(2,1)} %broadcast_in_dim.29), calls=%async_computation.1 | async-start | bytes 2097152 | tf_op jit(solution)/shard_map/all_to_all | solution.py:31
  183.1 6.9 %copy-start.2 = (f32[128,128]{1,0:T(8,128)S(1)}, f32[128,128]{1,0:T(8,128)}, u32[]{:S(2)}) copy-start(f32[128,128]{1,0:T(8,128)} %get-tuple-element.11) | copy-start | bytes 196612
  183.1 21.3 %copy-start.4 = (bf16[128,384]{1,0:T(8,128)(2,1)S(1)}, bf16[128,384]{1,0:T(8,128)(2,1)}, u32[]{:S(2)}) copy-start(bf16[128,384]{1,0:T(8,128)(2,1)} %get-tuple-element.10) | copy-start | bytes 294916
  186.1 10.8 %all-to-all-start.4 = ((f32[4,8,16,256]{3,2,1,0:T(8,128)}), f32[4,8,16,256]{3,2,1,0:T(8,128)S(1)}, u32[]{:S(2)}, u32[]{:S(2)}) async-start(f32[4,8,16,256]{3,2,1,0:T(8,128)} %bitcast.61), calls=%async_computation.4 | async-start | bytes 1048576 | tf_op jit(solution)/shard_map/all_to_all | solution.py:358
  197.6 14.9 %all-to-all-start.5 = ((f32[8,16,256]{2,1,0:T(8,128)}), f32[8,16,256]{2,1,0:T(8,128)S(1)}, u32[]{:S(2)}, u32[]{:S(2)}) async-start(f32[8,16,256]{2,1,0:T(8,128)} %reduce_sum.35), calls=%async_computation.5 | async-start | bytes 262144 | tf_op jit(solution)/shard_map/all_to_all | solution.py:359
  207.1 11.6 %copy-start.3 = (bf16[128,128]{1,0:T(8,128)(2,1)S(1)}, bf16[128,128]{1,0:T(8,128)(2,1)}, u32[]{:S(2)}) copy-start(bf16[128,128]{1,0:T(8,128)(2,1)} %get-tuple-element.9) | copy-start | bytes 98308
  212.4 30.8 %all-to-all-start.3 = ((bf16[16,128,256]{2,1,0:T(8,128)(2,1)}), bf16[16,128,256]{2,1,0:T(8,128)(2,1)S(1)}, u32[]{:S(2)}, u32[]{:S(2)}) async-start(bf16[16,128,256]{2,1,0:T(8,128)(2,1)} %bitcast.58), calls=%async_computation.3 | async-start | bytes 2097152 | tf_op jit(solution)/shard_map/all_to_all | solution.py:55
  243.2 32.6 %all-to-all-start.2 = ((bf16[16,128,256]{2,1,0:T(8,128)(2,1)}), bf16[16,128,256]{2,1,0:T(8,128)(2,1)S(1)}, u32[]{:S(2)}, u32[]{:S(2)}) async-start(bf16[16,128,256]{2,1,0:T(8,128)(2,1)} %bitcast.60), calls=%async_computation.2 | async-start | bytes 2097152 | tf_op jit(solution)/shard_map/all_to_all | solution.py:55
Sparse Core Ops, SparseCore 0:
  22.9 80.7 all-gather.1

commit v2 on v1

--- a/solution.py
+++ b/solution.py
@@ -1,5 +1,3 @@
-import math
-
 import jax
 import jax.numpy as jnp
 from jax import lax
@@ -18,42 +16,6 @@
 GELU_CUBIC = 0.044715
 CONTRACT_LAST = (((1,), (1,)), ((), ()))
 CONTRACT_FIRST = (((0,), (0,)), ((), ()))
-
-
-def joined_along(parts, dim):
-    parts = jnp.moveaxis(parts, 0, dim)
-    lengths = parts.shape
-    return parts.reshape(*lengths[:dim], lengths[dim] * lengths[dim + 1], *lengths[dim + 2 :])
-
-
-def from_everyone(array, axis):
-    copies = jnp.broadcast_to(array, (lax.axis_size(axis), *array.shape))
-    return lax.all_to_all(copies, axis, split_axis=0, concat_axis=0, tiled=True)
-
-
-def gather_directly(array, axis, dim):
-    return joined_along(from_everyone(array, axis), dim)
-
-
-def in_one_piece(arrays, axis, dim, along):
-    widths = [math.prod(a.shape[along:]) for a in arrays]
-    both = jnp.concatenate(
-        [a.reshape(*a.shape[:along], w) for a, w in zip(arrays, widths)], axis=along
-    )
-    out = lax.all_gather(both, axis, axis=dim, tiled=True)
-    parts = jnp.split(out, [sum(widths[:k]) for k in range(1, len(widths))], axis=along)
-    return tuple((b.reshape(*out.shape[:along], *a.shape[along:]) for a, b in zip(arrays, parts)))
-
-
-def in_blocks(array, dim, peers):
-    before, after = (array.shape[:dim], array.shape[dim + 1 :])
-    return jnp.moveaxis(array.reshape(*before, peers, -1, *after), dim, 0)
-
-
-def summed_on_arrival(array, axis, dim):
-    peers = lax.axis_size(axis)
-    parts = lax.all_to_all(in_blocks(array, dim, peers), axis, 0, 0, tiled=True)
-    return jnp.sum(parts.astype(jnp.float32), axis=0)
 
 
 def matmul(left, right):
@@ -100,33 +62,251 @@
     return centred * inv_scale, inv_scale
 
 
-def inner_kernel(
-    q_ref, k_ref, t_ref, e_ref, chunk_ref, dt_ref, w1_ref, w2_ref,
-    out_ref, dproj_ref, dlogit_ref, dw1_ref, dw2_ref,
+def layer_kernel(
+    tok_ref, wqkv_ref, wlr_ref, wout_ref, w1_ref, w2_ref, dout_ref,
+    out_ref, dtok_ref, share1_ref, share2_ref,
+    feat, cot, wq, wo, q_ref, k_ref, t_ref, e_ref, dt_ref, chunk_ref, ttt_ref, dproj_ref, dlogit_ref,
+    dw1_ref, dw2_ref, send_out, recv_out, send_tok, recv_tok, dw_send, dw_recv, dw_sum, share,
     chunks, s1, s2, in1, in2, snd1, snd2, w1b, w2b,
     sv_wide, sv_x2, sv_narrow, sv_kt, sv_x2t, sv_eg1, b_w1, b_w2,
+    near_send, feat_recv, cot_send, cot_recv, wq_recv, wq_recv_low, wo_recv, wo_recv_low,
     chunk_send, chunk_recv, hop_send, hop_recv,
+    out_send, out_recv, tok_send, tok_recv, dw_sems, dw_recvs, share_send, share_recv,
 ):
-    place = lax.axis_index("seq")
-    count = lax.axis_size("seq")
+    place, head, group = (lax.axis_index(name) for name in ("seq", "head", "dp"))
+    count, heads, groups = (lax.axis_size(name) for name in ("seq", "head", "dp"))
+    rows = tok_ref.shape[0]
+    half = rows // 2
     barrier = pltpu.get_barrier_semaphore()
 
-    def greet(step, carry):
-        pl.semaphore_signal(
-            barrier, inc=1, device_id={"seq": lax.rem(place + step, count)}, device_id_type=MESH
+    def greet_along(name, mine, size):
+        def greet(step, carry):
+            peer = lax.rem(mine + step, size)
+            pl.semaphore_signal(barrier, inc=1, device_id={name: peer}, device_id_type=MESH)
+            return carry
+
+        lax.fori_loop(1, size, greet, 0)
+
+    greet_along("seq", place, count)
+    greet_along("head", head, heads)
+    greet_along("dp", group, groups)
+    pl.semaphore_wait(barrier, count + heads + groups - 3)
+
+    started = []
+
+    def push(src, dst, arrival, device):
+        copy = pltpu.make_async_remote_copy(
+            src_ref=src,
+            dst_ref=dst,
+            send_sem=near_send.at[len(started)],
+            recv_sem=arrival,
+            device_id=device,
+            device_id_type=MESH,
         )
+        copy.start()
+        started.append(copy)
+
+    def arrived(dst, arrival):
+        pltpu.make_async_remote_copy(
+            src_ref=dst,
+            dst_ref=dst,
+            send_sem=near_send.at[0],
+            recv_sem=arrival,
+            device_id={"seq": place},
+            device_id_type=MESH,
+        ).wait_recv()
+
+    ring = heads // 2
+    ring_at, ring_base = lax.rem(head, ring), lax.div(head, ring) * ring
+    other_base = ring - ring_base
+    ring_up = {"head": ring_base + lax.rem(ring_at + 1, ring)}
+    ring_down = {"head": ring_base + lax.rem(ring_at + ring - 1, ring)}
+
+    def feat_push(block, device, src=None):
+        push(feat.at[block] if src is None else src, feat.at[block], feat_recv.at[block], device)
+
+    def feat_step(base, step):
+        below = base + lax.rem(ring_at + ring - step, ring)
+        arrived(feat.at[below], feat_recv.at[below])
+        if step < ring // 2:
+            feat_push(below, ring_up)
+            above = base + lax.rem(ring_at + step, ring)
+            arrived(feat.at[above], feat_recv.at[above])
+            if step < ring // 2 - 1:
+                feat_push(above, ring_down)
+
+    sib = place + 1 - 2 * lax.rem(place, 2)
+    sibling = {"seq": sib}
+    deep = [lax.rem(place + 2 * step, count) for step in range(4)]
+    sib_deep = [lax.rem(sib + 2 * step, count) for step in range(4)]
+    wide = [lax.rem(group + step, groups) for step in range(4)]
+    deep_up, deep_down = {"seq": deep[1]}, {"seq": deep[3]}
+    wide_up, wide_down = {"dp": wide[1]}, {"dp": wide[3]}
+
+    def wq_push(block, device, src=None):
+        push(wq.at[block] if src is None else src, wq.at[block], wq_recv.at[block], device)
+
+    def wq_relay(from_below, from_above, up, down):
+        push(wq.at[from_below, :half], wq.at[from_below, :half], wq_recv.at[from_below], up)
+        push(wq.at[from_above, half:], wq.at[from_above, half:], wq_recv_low.at[from_above], down)
+
+    def wq_arrived(block):
+        arrived(wq.at[block], wq_recv.at[block])
+
+    def wq_halves_arrived(block):
+        arrived(wq.at[block, :half], wq_recv.at[block])
+        arrived(wq.at[block, half:], wq_recv_low.at[block])
+
+    def wq_spread(row, src=None):
+        block = row * groups + group
+        wq_push(block, wide_up, src)
+        wq_push(block, wide_down, src)
+        wq_push(block, sibling, src)
+
+    def wq_sides(row):
+        below, above = row * groups + wide[3], row * groups + wide[1]
+        wq_arrived(below)
+        wq_arrived(above)
+        wq_relay(below, above, wide_up, wide_down)
+        wq_push(below, sibling)
+        wq_push(above, sibling)
+
+    def wq_far(row):
+        block = row * groups + wide[2]
+        wq_halves_arrived(block)
+        wq_push(block, sibling)
+
+    own = place * groups + group
+    feat_push(head, ring_up, tok_ref)
+    feat_push(head, ring_down, tok_ref)
+    partner = other_base + ring_at
+    feat_push(head, {"head": partner}, tok_ref)
+    wq_push(own, deep_up, wqkv_ref)
+    wq_push(own, deep_down, wqkv_ref)
+    wq_spread(place, wqkv_ref)
+    push(wout_ref, wo.at[own], wo_recv.at[own], wide_up)
+    push(wout_ref, wo.at[own], wo_recv.at[own], wide_down)
+    feat[head] = tok_ref[...]
+    cot[head] = dout_ref[...]
+    wq[own] = wqkv_ref[...]
+    wo[own] = wout_ref[...]
+    s1[...] = w1_ref[...]
+    s2[...] = w2_ref[...]
+
+    arrived(feat.at[partner], feat_recv.at[partner])
+    feat_push(partner, ring_up)
+    feat_push(partner, ring_down)
+    below, above = place * groups + wide[3], place * groups + wide[1]
+    arrived(wo.at[below], wo_recv.at[below])
+    arrived(wo.at[above], wo_recv.at[above])
+    push(wo.at[below, :half], wo.at[below, :half], wo_recv.at[below], wide_up)
+    push(wo.at[above, half:], wo.at[above, half:], wo_recv_low.at[above], wide_down)
+    feat_step(ring_base, 1)
+    wq_sides(place)
+    feat_step(other_base, 1)
+    far = place * groups + wide[2]
+    arrived(wo.at[far, :half], wo_recv.at[far])
+    arrived(wo.at[far, half:], wo_recv_low.at[far])
+
+    def wo_rows(row):
+        return pl.ds(row * groups, groups)
+
+    def wo_push(row, device):
+        push(wo.at[wo_rows(row)], wo.at[wo_rows(row)], wo_recv.at[count * groups + row], device)
+
+    def wo_arrived(row):
+        arrived(wo.at[wo_rows(row)], wo_recv.at[count * groups + row])
+
+    for row in (deep[3], deep[1]):
+        wq_arrived(row * groups + group)
+    wq_relay(deep[3] * groups + group, deep[1] * groups + group, deep_up, deep_down)
+    wq_spread(deep[3])
+    wq_spread(deep[1])
+    wo_push(place, deep_up)
+    wo_push(place, deep_down)
+    wo_push(place, sibling)
+    feat_step(ring_base, 2)
+    feat_step(other_base, 2)
+    wq_far(place)
+    feat_step(ring_base, 3)
+    feat_step(other_base, 3)
+
+    def cot_copy(step, source):
+        return pltpu.make_async_remote_copy(
+            src_ref=dout_ref,
+            dst_ref=cot.at[source],
+            send_sem=cot_send.at[step],
+            recv_sem=cot_recv.at[source],
+            device_id={"head": lax.rem(head + step, heads)},
+            device_id_type=MESH,
+        )
+
+    def cot_start(step, carry):
+        cot_copy(step, head).start()
         return carry
 
-    lax.fori_loop(1, count, greet, 0)
-    pl.semaphore_wait(barrier, count - 1)
-
-    def chunk_copy(source, target):
+    lax.fori_loop(1, heads, cot_start, 0)
+    wq_halves_arrived(deep[2] * groups + group)
+    wq_spread(deep[2])
+    wq_sides(deep[3])
+    wq_sides(deep[1])
+    wo_arrived(deep[3])
+    wo_arrived(deep[1])
+    low, high = deep[3] * groups, deep[1] * groups
+    pair = groups // 2
+    push(wo.at[pl.ds(low, pair)], wo.at[pl.ds(low, pair)], wo_recv.at[count * groups + deep[3]], deep_up)
+    push(
+        wo.at[pl.ds(high + pair, pair)], wo.at[pl.ds(high + pair, pair)],
+        wo_recv_low.at[count * groups + deep[1]], deep_down,
+    )
+    wo_push(deep[3], sibling)
+    wo_push(deep[1], sibling)
+    wq_sides(deep[2])
+    feat_step(ring_base, 4)
+    feat_step(other_base, 4)
+    wq_far(deep[3])
+    wq_far(deep[1])
+    wq_far(deep[2])
+    low = deep[2] * groups
+    arrived(wo.at[pl.ds(low, pair)], wo_recv.at[count * groups + deep[2]])
+    arrived(wo.at[pl.ds(low + pair, pair)], wo_recv_low.at[count * groups + deep[2]])
+    wo_push(deep[2], sibling)
+    for row in sib_deep:
+        for column in (0, 1, 3, 2):
+            wq_arrived(row * groups + wide[column])
+
+    def depth_rows(buffer, piece):
+        both = buffer[pl.ds(2 * piece, 2)]
+        return both.reshape(2 * rows, both.shape[-1])
+
+    def project(piece, carry):
+        total, logit = carry
+        part = feat[piece]
+        total = total + jnp.dot(part, depth_rows(wq, piece), preferred_element_type=F32)
+        weights = jnp.broadcast_to(wlr_ref[pl.ds(piece, 1), :], (HD, 2 * rows)).astype(BF16)
+        return total, logit + matmul_last(part, weights)
+
+    projected, logit = lax.fori_loop(
+        0, heads, project, (jnp.zeros((rows, 3 * HD), F32), jnp.zeros((rows, HD), F32)), unroll=4
+    )
+    keys = projected[:, HD : 2 * HD]
+    target = projected[:, 2 * HD :] - keys
+    rates = (BASE_RATE / HD) * jax.nn.sigmoid(logit)
+    chunk_ref[:, :HD] = keys.astype(BF16)
+    chunk_ref[:, HD : 2 * HD] = target.astype(BF16)
+    chunk_ref[:, 2 * HD :] = rates.astype(BF16)
+    q_ref[...] = projected[:, :HD]
+    k_ref[...] = keys
+    t_ref[...] = target
+    e_ref[...] = rates
+
+    def chunk_copy(source, to):
         return pltpu.make_async_remote_copy(
             src_ref=chunk_ref,
             dst_ref=chunks.at[source],
-            send_sem=chunk_send.at[target],
+            send_sem=chunk_send.at[to],
             recv_sem=chunk_recv.at[source],
-            device_id={"seq": target},
+            device_id={"seq": to},
             device_id_type=MESH,
         )
 
@@ -135,9 +315,6 @@
         return carry
 
     lax.fori_loop(0, count - 1 - place, send_chunk, 0)
-
-    s1[...] = w1_ref[...]
-    s2[...] = w2_ref[...]
 
     def replay_block(k, t, e):
         first, second = s1[...].astype(BF16), s2[...].astype(BF16)
@@ -159,6 +336,20 @@
         return carry
 
     lax.fori_loop(0, place, replay_turn, 0)
+
+    for row in sib_deep:
+        wo_arrived(row)
+
+    def gather_cotangent(step, total):
+        source = lax.rem(head + step, heads)
+
+        @pl.when(step > 0)
+        def _():
+            cot_copy(0, source).wait_recv()
+
+        return total + jnp.dot(cot[source], depth_rows(wo, source), preferred_element_type=F32)
+
+    dt_ref[...] = lax.fori_loop(0, heads, gather_cotangent, jnp.zeros((rows, HD), F32))
 
     place_row = lax.broadcasted_iota(jnp.int32, (MB, MB), 0)
     place_col = lax.broadcasted_iota(jnp.int32, (MB, MB), 1)
@@ -193,7 +384,7 @@
         raw2 = matmul_last(xq, x2)
         a2 = raw2 * causal
         nq, sq = norm_rows(matmul(xq, second) - matmul(a2, g2))
-        out_ref[span, :] = (q + nq).astype(BF16)
+        ttt_ref[span, :] = (q + nq).astype(BF16)
         do = dt_ref[span, :]
         dyq = sq * (do - row_mean(do) - nq * row_mean(do * nq))
         da2 = -matmul_last(dyq, g2)
@@ -226,6 +417,37 @@
         sv_narrow[block, 7] = jnp.broadcast_to(s, (MB, HD))
         sv_narrow[block, 8] = jnp.broadcast_to(cross, (MB, HD))
         sv_narrow[block, 9] = eg2
+
+    def share_out(step, source):
+        to = lax.rem(head + step, heads)
+        return pltpu.make_async_remote_copy(
+            src_ref=send_out.at[to],
+            dst_ref=recv_out.at[source],
+            send_sem=out_send.at[to],
+            recv_sem=out_recv.at[source],
+            device_id={"head": to},
+            device_id_type=MESH,
+        )
+
+    def send_terms():
+        def one(step, carry):
+            to = lax.rem(head + step, heads)
+            term = matmul_last(ttt_ref[...], depth_rows(wo, to)).astype(BF16)
+            send_out[to] = term
+
+            @pl.when(step > 1)
+            def _():
+                share_out(step - 1, head).start()
+
+            return carry
+
+        lax.fori_loop(1, heads, one, 0)
+        recv_out[head] = matmul_last(ttt_ref[...], depth_rows(wo, head)).astype(BF16)
+        share_out(heads - 1, head).start()
+
+    @pl.when(place < count - 1)
+    def _():
+        send_terms()
 
     def hop(target, which):
         return pltpu.make_async_remote_copy(
@@ -294,35 +516,173 @@
         dproj_ref[span, 2 * HD :] = (-dr).astype(BF16)
         dlogit_ref[span, :] = de * e * (1.0 - e * (HD / BASE_RATE))
 
+    @pl.when(place == count - 1)
+    def _():
+        send_terms()
+
+    def share_tok(step, source):
+        to = lax.rem(head + step, heads)
+        return pltpu.make_async_remote_copy(
+            src_ref=send_tok.at[to],
+            dst_ref=recv_tok.at[source],
+            send_sem=tok_send.at[to],
+            recv_sem=tok_recv.at[source],
+            device_id={"head": to},
+            device_id_type=MESH,
+        )
+
+    def token_term(to):
+        term = matmul_last(dproj_ref[...], depth_rows(wq, to))
+        d_logit = dlogit_ref[...]
+        both = jnp.concatenate([d_logit, d_logit], axis=1)
+        return (term + both * wlr_ref[pl.ds(to, 1), :]).astype(BF16)
+
+    def send_token_term(step, carry):
+        to = lax.rem(head + step, heads)
+        send_tok[to] = token_term(to)
+
+        @pl.when(step > 1)
+        def _():
+            share_tok(step - 1, head).start()
+
+        return carry
+
+    lax.fori_loop(1, heads, send_token_term, 0)
+    recv_tok[head] = token_term(head)
+    share_tok(heads - 1, head).start()
+
+    def dw_copy(step, source):
+        to = lax.rem(group + step, groups)
+        return pltpu.make_async_remote_copy(
+            src_ref=dw_send.at[to],
+            dst_ref=dw_recv.at[source],
+            send_sem=dw_sems.at[step],
+            recv_sem=dw_recvs.at[source],
+            device_id={"dp": to},
+            device_id_type=MESH,
+        )
+
+    def share_copy(to):
+        return pltpu.make_async_remote_copy(
+            src_ref=dw_sum.at[to],
+            dst_ref=share,
+            send_sem=share_send.at[to],
+            recv_sem=share_recv,
+            device_id={"seq": to},
+            device_id_type=MESH,
+        )
+
+    @pl.when(place == 0)
+    def _():
+        joined = jnp.concatenate([jnp.transpose(dw1_ref[...]), dw2_ref[...]], axis=1)
+        parts = joined.reshape(count, groups, -1, 2 * HD)
+        for part in range(groups):
+            dw_send[part] = parts[:, part]
+        for step in range(1, groups):
+            dw_copy(step, group).start()
+        total = dw_send[group]
+        for step in range(1, groups):
+            source = lax.rem(group + step, groups)
+            dw_copy(step, source).wait_recv()
+            total = total + dw_recv[source]
+        dw_sum[...] = total
+        share[...] = total[0]
+        for to in range(1, count):
+            share_copy(to).start()
+
+    def sum_terms(copy, received):
+        def add(step, total):
+            source = lax.rem(head + step, heads)
+
+            @pl.when(step > 0)
+            def _():
+                copy(0, source).wait_recv()
+
+            return total + received[source].astype(F32)
+
+        return lax.fori_loop(0, heads, add, jnp.zeros((rows, 2 * HD), F32)).astype(BF16)
+
+    out_ref[...] = sum_terms(share_out, recv_out)
+    dtok_ref[...] = sum_terms(share_tok, recv_tok)
+
+    @pl.when(place > 0)
+    def _():
+        share_copy(0).wait_recv()
+
+    share1_ref[...] = jnp.transpose(share[:, :HD])
+    share2_ref[...] = share[:, HD:]
+
     @pl.when(place > 0)
     def _():
         hop(place - 1, 0).wait_send()
         hop(place - 1, 1).wait_send()
 
+    @pl.when(place == 0)
+    def _():
+        for step in range(1, groups):
+            dw_copy(step, group).wait_send()
+        for to in range(1, count):
+            share_copy(to).wait_send()
+
     def sent_chunk(step, carry):
         chunk_copy(place, count - 1 - step).wait_send()
         return carry
 
     lax.fori_loop(0, count - 1 - place, sent_chunk, 0)
 
-
-def inner_layer(q, k, t, e, chunk, d_ttt, w_first, w_second):
-    rows = q.shape[0]
-    peers = lax.axis_size("seq")
+    def sent_terms(step, carry):
+        share_out(step, head).wait_send()
+        share_tok(step, head).wait_send()
+        cot_copy(step, head).wait_send()
+        return carry
+
+    lax.fori_loop(1, heads, sent_terms, 0)
+    for copy in started:
+        copy.wait_send()
+
+
+def layer(tokens, w_qkv, w_lr, w_out, w_first, w_second, d_out):
+    rows, width = tokens.shape
+    peers, heads, groups = (lax.axis_size(name) for name in ("seq", "head", "dp"))
     inner = w_first.shape[1]
+    share = inner // (peers * groups)
+    blocks = peers * groups
     vmem = pl.BlockSpec(memory_space=pltpu.VMEM)
+    dma = pltpu.SemaphoreType.DMA
     return pl.pallas_call(
-        inner_kernel,
+        layer_kernel,
         out_shape=(
-            jax.ShapeDtypeStruct((rows, HD), BF16),
-            jax.ShapeDtypeStruct((rows, 3 * HD), BF16),
-            jax.ShapeDtypeStruct((rows, HD), F32),
-            jax.ShapeDtypeStruct((HD, inner), F32),
-            jax.ShapeDtypeStruct((inner, HD), F32),
+            jax.ShapeDtypeStruct((rows, width), BF16),
+            jax.ShapeDtypeStruct((rows, width), BF16),
+            jax.ShapeDtypeStruct((HD, share), F32),
+            jax.ShapeDtypeStruct((share, HD), F32),
         ),
-        in_specs=[vmem] * 8,
-        out_specs=(vmem,) * 5,
+        in_specs=[vmem] * 7,
+        out_specs=(vmem,) * 4,
         scratch_shapes=[
+            pltpu.VMEM((heads, rows, width), BF16),
+            pltpu.VMEM((heads, rows, width), BF16),
+            pltpu.VMEM((blocks, rows, 3 * HD), BF16),
+            pltpu.VMEM((blocks, rows, HD), BF16),
+            pltpu.VMEM((rows, HD), F32),
+            pltpu.VMEM((rows, HD), F32),
+            pltpu.VMEM((rows, HD), F32),
+            pltpu.VMEM((rows, HD), F32),
+            pltpu.VMEM((rows, HD), F32),
+            pltpu.VMEM((rows, 3 * HD), BF16),
+            pltpu.VMEM((rows, HD), BF16),
+            pltpu.VMEM((rows, 3 * HD), BF16),
+            pltpu.VMEM((rows, HD), F32),
+            pltpu.VMEM((HD, inner), F32),
+            pltpu.VMEM((inner, HD), F32),
+            pltpu.VMEM((heads, rows, width), BF16),
+            pltpu.VMEM((heads, rows, width), BF16),
+            pltpu.VMEM((heads, rows, width), BF16),
+            pltpu.VMEM((heads, rows, width), BF16),
+            pltpu.VMEM((groups, peers, share, 2 * HD), F32),
+            pltpu.VMEM((groups, peers, share, 2 * HD), F32),
+            pltpu.VMEM((peers, share, 2 * HD), F32),
+            pltpu.VMEM((share, 2 * HD), F32),
             pltpu.VMEM((peers, rows, 3 * HD), BF16),
             pltpu.VMEM((HD, inner), F32),
             pltpu.VMEM((inner, HD), F32),
@@ -340,52 +700,44 @@
             pltpu.VMEM((2, MB, inner), BF16),
             pltpu.VMEM((2, HD, inner), F32),
             pltpu.VMEM((2, inner, HD), F32),
-            pltpu.SemaphoreType.DMA((peers,)),
-            pltpu.SemaphoreType.DMA((peers,)),
-            pltpu.SemaphoreType.DMA((2,)),
-            pltpu.SemaphoreType.DMA((2,)),
+            dma((64,)),
+            dma((heads,)),
+            dma((heads,)),
+            dma((heads,)),
+            dma((blocks,)),
+            dma((blocks,)),
+            dma((blocks + peers,)),
+            dma((blocks + peers,)),
+            dma((peers,)),
+            dma((peers,)),
+            dma((2,)),
+            dma((2,)),
+            dma((heads,)),
+            dma((heads,)),
+            dma((heads,)),
+            dma((heads,)),
+            dma((groups,)),
+            dma((groups,)),
+            dma((peers,)),
+            dma(()),
         ],
         compiler_params=pltpu.CompilerParams(collective_id=0, has_side_effects=True),
-        name="inner_layer",
-    )(q, k, t, e, chunk, d_ttt, w_first, w_second)
-
-
-def gradient_shares(first, second):
-    peers, groups = lax.axis_size("seq"), lax.axis_size("dp")
-    both = jnp.concatenate([first.transpose(1, 0), second], axis=1)
-    width = both.shape[1]
-    parts = both.reshape(peers, groups, -1, width).transpose(1, 0, 2, 3)
-    summed = jnp.sum(lax.all_to_all(parts, "dp", 0, 0, tiled=True), axis=0)
-    own = lax.all_to_all(summed, "seq", 0, 0, tiled=True)[0]
-    return own[:, :HD].transpose(1, 0)[None], own[:, HD:][None]
+        name="layer",
+    )(tokens, w_qkv, w_lr, w_out, w_first, w_second, d_out)
 
 
 def body(tokens, w_qkv, w_lr, w_out, w1_init, w2_init, d_out):
-    head_width = w_qkv.shape[2]
-    features = gather_directly(tokens[0], "head", 1)
-    part_qkv, part_out = in_one_piece((w_qkv, w_out), "dp", 0, 1)
-    wide_qkv, wide_out = in_one_piece((part_qkv, part_out), "seq", 0, 1)
-    full_depth = wide_qkv.shape[0]
-    qkv_matrix = wide_qkv.reshape(full_depth, 3 * head_width)
-    projected = jnp.dot(features, qkv_matrix, preferred_element_type=F32)
-    rate_logit = jnp.dot(features, w_lr, preferred_element_type=F32)
-    queries = projected[:, :head_width]
-    key_rows = projected[:, head_width : 2 * head_width]
-    target = projected[:, 2 * head_width :] - key_rows
-    rates = jnp.broadcast_to(BASE_RATE * jax.nn.sigmoid(rate_logit) / head_width, target.shape)
-    chunk = jnp.concatenate([key_rows, target, rates], axis=1).astype(BF16)
-    d_full = gather_directly(d_out[0], "head", 1)
-    d_ttt = jnp.dot(d_full, wide_out, preferred_element_type=F32)
-    ttt_out, d_proj, d_logit, d_first, d_second = inner_layer(
-        queries, key_rows, target, rates, chunk, d_ttt, w1_init[0], w2_init[0]
+    depth, parts, width = w_qkv.shape
+    out, d_tokens, share_first, share_second = layer(
+        tokens[0],
+        w_qkv.reshape(depth, parts * width),
+        w_lr.astype(F32).reshape(lax.axis_size("head"), -1),
+        w_out,
+        w1_init[0],
+        w2_init[0],
+        d_out[0],
     )
-    out_term = lax.dot_general(ttt_out, wide_out, CONTRACT_LAST, preferred_element_type=F32)
-    out = summed_on_arrival(out_term.astype(BF16), "head", 1).astype(BF16)[None]
-    grad_term = lax.dot_general(d_proj, qkv_matrix, CONTRACT_LAST, preferred_element_type=F32)
-    grad_term = grad_term + d_logit[:, :1] * w_lr[:, 0].astype(F32)[None, :]
-    d_tokens = summed_on_arrival(grad_term.astype(BF16), "head", 1).astype(BF16)[None]
-    share_first, share_second = gradient_shares(d_first, d_second)
-    return (out, d_tokens, share_first, share_second)
+    return (out[None], d_tokens[None], share_first[None], share_second[None])
 
 
 def solution(mesh):

time: 285 us -> 160 us (0.56)
  waiting for transfers between devices: 120 us -> 0 us
  Pallas kernels: 72 us -> 150 us
  starting transfers between devices: 38.8 us -> 0 us
  blocking collectives: 13.7 us -> 0 us
  between operations: 14.2 us -> 0.66 us
  matrix products: 9.77 us -> 0 us
  local copies, waits for them, and re-layouts: 10.9 us -> 6.06 us
  other arithmetic: 4.63 us -> 0.76 us
    all_to_all x6 -> x0, waiting for transfers between devices: 80.5 us -> none  [the longest x2 46 us: summed_on_arrival(): parts = lax.all_to_all(in_blocks(array, dim, peers), axis, 0, 0, tiled=True)]
    pallas_call x1, Pallas kernels: 72 us -> 150 us  [layer(): pl.pallas_call(layer_kernel, out_shape=(jax.ShapeDtypeStruct((rows, width...]
    all_gather x1 -> x0, waiting for transfers between devices: 39 us -> none  [in_one_piece(): out = lax.all_gather(both, axis, axis=dim, tiled=True)]
    all_to_all x6 -> x0, starting transfers between devices: 38.7 us -> none  [the longest x2 14.8 us: from_everyone(): return lax.all_to_all(copies, axis, split_axis=0, concat_axis=0, tiled=True)]
    all_gather x1 -> x0, blocking collectives: 13.7 us -> none  [in_one_piece(): out = lax.all_gather(both, axis, axis=dim, tiled=True)]
    dot_general x5 -> x0, matrix products: 9.77 us -> none  [the longest x1 2.88 us: body(): projected = jnp.dot(features, qkv_matrix, preferred_element_type=F32)]
    broadcast_in_dim x5 -> x0, local copies, waits for them, and re-layouts: 3.71 us -> none  [the longest x2 2.33 us: from_everyone(): copies = jnp.broadcast_to(array, (lax.axis_size(axis), *array.shape))]
  transfers between devices with their start and end apart: 7 -> 0, of which waited for: 6 -> 0; matrix products, arithmetic and copies ran while one was open for 6% -> 0% of each run, Pallas kernels for 0% -> 0%
where the time goes in v2:
time: 160 us; the launch traced here: 157 us
  Pallas kernels  150 us (94%)
  local copies, waits for them, and re-layouts  6.06 us (4%)
    pallas_call x1, Pallas kernels, layer(): pl.pallas_call(layer_kernel, out_shape=(jax.ShapeDtypeStruct((rows, width...  150 us
    unnamed x11, local copies, waits for them, and re-layouts  4.71 us

profile of v2, /device:TPU:1, one launch (start us, length us, event | category | flops | bytes accessed | tf_op | source)
XLA Modules:
  0.0 157.1 jit_solution(5035307123398810094)
XLA Ops:
  0.6 0.8 convert_reduce_fusion
  1.4 0.6 reshape.20.wlr_ref
  2.0 1.0 copy.13
  3.0 0.7 copy.14.wqkv_ref
  3.8 149.7 %layer.1 = (bf16[128,256]{1,0:T(8,128)(2,1)}, bf16[128,256]{1,0:T(8,128)(2,1)}, f32[128,16]{1,0:T(8,128)}, f32[16,128]{1,0:T(8,128)}) custom-call(bf16[128,256]{1,0:T(8,128)(2,1)} %bitcast.12, bf16[128,384]{1,0:T(8,128)(2,1)} %copy.14.wqkv_ref, f32[16,256]{1,0:T(8,128)} %reshape.20.wlr_ref, bf16[128,128]{1,0:T(8,128)(2,1)} %wout_ref.1, f32[128,512]{1,0:T(8,128)} %bitcast.10, ...), custom_call_target="tpu_custom_call" | custom-call | tf_op jit(solution)/shard_map/layer/pallas_call | solution.py:652
  153.4 0.0 copy-start.1
  153.4 1.5 copy.15
  155.0 0.0 copy-done.1
  155.0 0.0 copy-start
  155.0 0.6 copy.19
  155.6 0.2 copy-done
  155.8 0.0 copy-start.2
  155.8 0.6 copy.20
  156.5 0.1 copy-done.2
  156.5 0.6 copy.21
Async XLA Ops:
  153.4 1.6 copy-start.1
  155.0 0.9 copy-start
  155.8 0.7 copy-start.2
